TPU v7x, 512 devices: a whole 4x4x16 slice. The times are simulated.
512 devices in a mesh: group: 16 (over y, x), member: 32 (over z, core).
Axes of the slice: x: 4, y: 4, z: 16, core: 2. Of those that a mesh axis runs over, the one named last changes fastest.
Arguments:
- amplitudes: bfloat16 [8192, 128, 128], P(('group', 'member')), may hold values from -6 to 6
- integrals: bfloat16 [4096, 128, 128], P(('group', 'member')), may hold values from -0.02734375 to 0.02734375
- tasks: int32 [196608, 3], P(('group', 'member')), may hold values from 0 to 63, as said below
- requests: int32 [8192, 4], P(('group', 'member')), may hold values from 0 to 7
- counts: int32 [512], P(('group', 'member')), may hold values from 1 to 384, as said below
Outputs:
- residual: float32 [512, 128, 128], P(('group', 'member'))
Inputs may be any that keep to these rules, and one draw needn't show every extreme that they name: `tasks`: column 0 is below 16, column 1 below 64, column 2 below 32; slots beyond a device's count hold valid entries too. `counts`: some device has 384 live tasks in every draw.
All inputs are finite; a program needn't handle non-finite values.
Results may differ from a plain program's by a relative error of at most 0.0003.
Values may be sent and summed in bfloat16 or wider, within the bound.
No kernel may reach another device: no remote copies, remote signals or barrier semaphores. Data moves between devices by JAX's collectives and lax.ppermute only.
A program may use at most 64 MiB of HBM per device.

v0:
```python
import jax
import jax.numpy as jnp
from jax import lax
from jax.sharding import Mesh
from jax.sharding import PartitionSpec as P

RES_DEV = 1
MEMBER = ("member_0", "member_1")
GROUP_MEMBER = ("group", "member_0", "member_1")


block_rows = 16


def own_block(pieces, axes, turns):
    dims = [lax.axis_size(a) for a in axes]
    pieces = pieces.reshape(*dims, *pieces.shape[1:])
    pieces = pieces.transpose(*turns, *range(len(axes), pieces.ndim))
    pieces = pieces.reshape(-1, *pieces.shape[len(axes) :])
    for k in turns:
        pieces = lax.psum_scatter(pieces, axes[k], scatter_dimension=0, tiled=True)
    return pieces[0]


def in_blocks(shard, dim, peers):
    dims = shard.shape
    pieces = shard.reshape(*dims[:dim], peers, dims[dim] // peers, *dims[dim + 1 :])
    return jnp.moveaxis(pieces, dim, 0)


def scatter_axes(shard, axes, turns, dim):
    peers = lax.axis_size(axes)
    return own_block(in_blocks(shard, dim, peers), axes, turns)


def accumulate(total, amps, fetched, task_list, lower, upper):
    capacity = task_list.shape[0]
    blocks = (upper - lower + block_rows - 1) // block_rows

    def block(k, running):
        index = lower + k * block_rows + jnp.arange(block_rows, dtype=jnp.int32)
        valid = index < upper
        rows = task_list[jnp.minimum(index, capacity - 1)]
        left = amps[rows[:, 0]]
        right = fetched[rows[:, 1]]
        product = jnp.einsum("kij,kjl->kil", left, right, preferred_element_type=jnp.float32)
        product = jnp.where(valid[:, None, None], product, jnp.zeros_like(product))
        return running.at[rows[:, 2]].add(product)

    return lax.fori_loop(0, blocks, block, total)


def per_device(amplitudes, integrals, tasks, requests, counts):
    tile = amplitudes.shape[1]
    fetched = lax.all_to_all(
        integrals[lax.all_to_all(requests, "group", split_axis=0, concat_axis=0, tiled=True)],
        "group",
        split_axis=0,
        concat_axis=0,
        tiled=True,
    )
    fetched = fetched.reshape(-1, tile, tile)
    total = jnp.zeros((RES_DEV * lax.axis_size(MEMBER), tile, tile), jnp.float32)
    mine = counts[0]
    total = accumulate(total, amplitudes, fetched, tasks, 0, mine)
    return scatter_axes(total, MEMBER, (1, 0), 0)


def solution(mesh):
    finer = Mesh(
        mesh.devices.reshape(mesh.shape["group"], 16, 2), ("group", "member_0", "member_1")
    )
    placed = (
        P(GROUP_MEMBER, None, None),
        P(GROUP_MEMBER, None, None),
        P(GROUP_MEMBER, None),
        P(GROUP_MEMBER, None),
        P(GROUP_MEMBER),
    )
    return jax.shard_map(
        per_device,
        mesh=finer,
        in_specs=placed,
        out_specs=P(GROUP_MEMBER, None, None),
        check_vma=False,
    )
```

profile of v0, /device:TPU:6, one launch (start us, length us, event | category | flops | bytes accessed | tf_op | source)
XLA Modules:
  0.0 357.3 jit_solution(6608801916382718419)
XLA Ops:
  6.5 0.8 copy.12
  7.3 13.9 %all_to_all.17 = s32[16,1,4]{2,1,0:T(1,128)S(1)} all-to-all(s32[16,1,4]{2,1,0:T(1,128)S(1)} %copy.12), channel_id=1, replica_groups=mesh['group'=16,'member_0'=16,'member_1'=2] {'group'}, dimensions={0} | all-to-all | bytes 512 | tf_op jit(solution)/shard_map/all_to_all | solution.py:56
  21.5 2.1 gather_fusion.3
  23.6 6.4 %all-to-all-start.1 = ((bf16[16,4,128,128]{3,2,1,0:T(8,128)(2,1)}), bf16[16,4,128,128]{3,2,1,0:T(8,128)(2,1)}, u32[]{:S(2)}, u32[]{:S(2)}) async-start(bf16[16,4,128,128]{3,2,1,0:T(8,128)(2,1)} %bitcast.3), calls=%async_computation.1 | async-start | bytes 4194304 | tf_op jit(solution)/shard_map/all_to_all | solution.py:55
  30.9 22.8 %all-to-all-done.1 = bf16[16,4,128,128]{3,2,1,0:T(8,128)(2,1)} async-done(((bf16[16,4,128,128]{3,2,1,0:T(8,128)(2,1)}), bf16[16,4,128,128]{3,2,1,0:T(8,128)(2,1)}, u32[]{:S(2)}, u32[]{:S(2)}) %all-to-all-start.1) | async-done | bytes 2097184 | tf_op jit(solution)/shard_map/all_to_all | solution.py:55
  53.7 1.5 broadcast_in_dim.7
  55.2 97.5 %while.10 = (s32[]{:T(128)}, f32[32,128,128]{2,1,0:T(8,128)}, s32[]{:T(128)}, s32[384,3]{1,0:T(8,128)S(1)}, s32[]{:T(128)}, /*index=5*/bf16[16,128,128]{2,1,0:T(...) while((s32[]{:T(128)}, f32[32,128,128]{2,1,0:T(8,128)}, s32[]{:T(128)}, ...), condition=%wide.region_2.3_spmd, body=%wide.region_0.2_spmd.sunk | while | flops 67636480 | bytes 7353749 | solution.py:50
  55.2 0.7 add_compare_fusion.2
  56.0 0.6 gather_fusion
  56.8 0.6 gather_fusion.1
  57.5 2.2 gather_fusion.2
  60.0 3.4 scatter_fusion
  63.4 0.7 add_compare_fusion.2
  64.2 0.6 gather_fusion
  65.0 0.6 gather_fusion.1
  65.7 2.2 gather_fusion.2
  68.2 3.3 scatter_fusion
  71.5 0.7 add_compare_fusion.2
  72.3 0.6 gather_fusion
  73.1 0.6 gather_fusion.1
  73.7 2.2 gather_fusion.2
  76.3 3.3 scatter_fusion
  79.6 0.7 add_compare_fusion.2
  80.4 0.6 gather_fusion
  81.2 0.6 gather_fusion.1
  81.9 2.2 gather_fusion.2
  84.4 3.4 scatter_fusion
  87.8 0.7 add_compare_fusion.2
  88.6 0.6 gather_fusion
  89.4 0.6 gather_fusion.1
  90.0 2.2 gather_fusion.2
  92.6 3.3 scatter_fusion
  95.9 0.7 add_compare_fusion.2
  97.5 0.6 gather_fusion.1
  98.1 2.2 gather_fusion.2
  100.7 3.3 scatter_fusion
  104.0 0.7 add_compare_fusion.2
  105.6 0.6 gather_fusion.1
  106.2 2.2 gather_fusion.2
  108.8 3.4 scatter_fusion
  112.1 0.7 add_compare_fusion.2
  113.7 0.6 gather_fusion.1
  114.4 2.2 gather_fusion.2
  116.9 3.3 scatter_fusion
  120.2 0.7 add_compare_fusion.2
  121.8 0.6 gather_fusion.1
  122.5 2.2 gather_fusion.2
  125.0 3.4 scatter_fusion
  128.4 0.7 add_compare_fusion.2
  130.0 0.6 gather_fusion.1
  130.6 2.2 gather_fusion.2
  133.2 3.4 scatter_fusion
  136.5 0.7 add_compare_fusion.2
  138.1 0.6 gather_fusion.1
  138.8 2.2 gather_fusion.2
  141.3 3.3 scatter_fusion
  144.6 0.7 add_compare_fusion.2
  145.4 0.6 gather_fusion
  146.2 0.6 gather_fusion.1
  146.9 2.2 gather_fusion.2
  149.4 3.3 scatter_fusion
  152.7 3.2 copy.16
  156.0 119.6 %reduce-scatter.3.cloned.1.call-done = f32[16,1,128,128]{3,2,1,0:T(8,128)} async-done(((f32[32,1,128,128]{3,2,1,0:T(8,128)}), f32[16,1,128,128]{3,2,1,0:T(8,128)}) %reduce-scatter.3.cloned.1.call-update) | async-done | bytes 1048592 | tf_op jit(solution)/shard_map/reduce_scatter | solution.py:21
  275.7 74.8 %reduce-scatter.5.cloned.1.call-done = f32[1,1,128,128]{3,2,1,0:T(8,128)} async-done(((f32[16,1,128,128]{3,2,1,0:T(8,128)}), f32[1,1,128,128]{3,2,1,0:T(8,128)}) %reduce-scatter.5.cloned.1.call-update) | async-done | bytes 65552 | tf_op jit(solution)/shard_map/reduce_scatter | solution.py:21
  (82 shorter events, 11.6 us)
Async XLA Ops:
  6.5 15.0 %copy-start = (bf16[8,128,128]{2,1,0:T(8,128)(2,1)S(1)}, bf16[8,128,128]{2,1,0:T(8,128)(2,1)}, u32[]{:S(2)}) copy-start(bf16[8,128,128]{2,1,0:T(8,128)(2,1)} %param.8) | copy-start | bytes 786436
  23.6 7.1 %copy-start.2 = (s32[384,3]{0,1:T(4,128)S(1)}, s32[384,3]{0,1:T(4,128)}, u32[]{:S(2)}) copy-start(s32[384,3]{0,1:T(4,128)} %param.9) | copy-start | bytes 13828
  23.6 30.1 %all-to-all-start.1 = ((bf16[16,4,128,128]{3,2,1,0:T(8,128)(2,1)}), bf16[16,4,128,128]{3,2,1,0:T(8,128)(2,1)}, u32[]{:S(2)}, u32[]{:S(2)}) async-start(bf16[16,4,128,128]{3,2,1,0:T(8,128)(2,1)} %bitcast.3), calls=%async_computation.1 | async-start | bytes 4194304 | tf_op jit(solution)/shard_map/all_to_all | solution.py:55
  30.0 25.3 %copy-start.1 = (bf16[16,128,128]{2,1,0:T(8,128)(2,1)S(1)}, bf16[16,128,128]{2,1,0:T(8,128)(2,1)}, u32[]{:S(2)}) copy-start(bf16[16,128,128]{2,1,0:T(8,128)(2,1)} %param.7) | copy-start | bytes 1572868
  30.0 245.6 %reduce-scatter.3.cloned.1.call-start = ((), (), s32[]{:S(2)}) async-start(), calls=%async_computation.4 | async-start | bytes 3145728 | tf_op jit(solution)/shard_map/reduce_scatter | solution.py:21
  155.9 194.5 %reduce-scatter.5.cloned.1.call-start = ((), (), s32[]{:S(2)}) async-start(), calls=%async_computation.5 | async-start | bytes 1114112 | tf_op jit(solution)/shard_map/reduce_scatter | solution.py:21
Sparse Core Ops, SparseCore 0:
  156.1 119.5 reduce-scatter.2
  278.7 71.7 reduce-scatter.4
where the time goes:
time: 360 us; the launch traced here: 357 us
  waiting for transfers between devices  217 us (60%)
  other arithmetic  52.1 us (14%)
  local copies, waits for them, and re-layouts  49.4 us (14%)
  between operations  14.2 us (4%)
  blocking collectives  13.9 us (4%)
  starting transfers between devices  6.45 us (2%)
    reduce_scatter x2, waiting for transfers between devices, own_block(): pieces = lax.psum_scatter(pieces, axes[k], scatter_dimension=0, tiled=True)  194 us
    scatter-add x12, other arithmetic, block(): return running.at[rows[:, 2]].add(product)  40.1 us
    gather x12, local copies, waits for them, and re-layouts, block(): right = fetched[rows[:, 1]]  26.9 us
    all_to_all x1, waiting for transfers between devices, per_device(): lax.all_to_all(integrals[lax.all_to_all(requests, 'group', split_axis=0,...  22.8 us
    all_to_all x1, blocking collectives, per_device(): lax.all_to_all(requests, 'group', split_axis=0, concat_axis=0, tiled=True)  13.9 us
    lt x12, other arithmetic, block(): valid = index < upper  7.8 us
    gather x12, local copies, waits for them, and re-layouts, block(): left = amps[rows[:, 0]]  7.77 us
  transfers between devices with their start and end apart: 3, of which 3 were waited for; matrix products, arithmetic and copies ran while one was open for 0% of the time, Pallas kernels for 0%

commit v1 on v0

v1 whole, which is shorter than its diff:
```python
import functools

import jax
import jax.numpy as jnp
from jax import lax
from jax.experimental import pallas as pl
from jax.experimental.pallas import tpu as pltpu
from jax.sharding import Mesh
from jax.sharding import PartitionSpec as P

GROUP_MEMBER = ("group", "z", "core")
PAIR = 2
UNROLL = 8
SLOTS = 512
TOP = 32760.0
STEPS = 128.0


def task_tables(tasks, counts, core, tiles):
    a, s, r = tasks.T
    half = tiles // 2
    k = jnp.arange(tasks.shape[0], dtype=jnp.int32)
    valid = k < counts[0]
    q = jnp.where(valid, ((r & 1) ^ core ^ 1) * half + (r >> 1), tiles)
    code = a + s * 32
    rank = jnp.sum(((q[:, None] == q[None, :]) & (k[None, :] < k[:, None])).astype(jnp.int32), 1)
    b = jnp.arange(tiles, dtype=jnp.int32)
    hot = q[:, None] == b[None, :]
    groups = (jnp.sum(hot.astype(jnp.int32), 0) + PAIR - 1) // PAIR
    ends = jnp.sum(jnp.where(b[:, None] <= b[None, :], groups[:, None], 0), 0)
    first = jnp.sum(jnp.where(hot, (ends - groups)[None, :], 0), 1)
    place = jnp.where(valid, first * PAIR + rank, -1)
    p = jnp.arange(SLOTS, dtype=jnp.int32)
    table = 16 + jnp.sum(jnp.where(place[:, None] == p[None, :], code[:, None] - 16, 0), 0)
    j = jnp.arange(SLOTS // PAIR, dtype=jnp.int32)
    target = jnp.sum((ends[:, None] <= j[None, :]).astype(jnp.int32), 0)
    bounds = jnp.stack([jnp.zeros_like(ends[0]), ends[half - 1], ends[tiles - 1]])
    return table, target, bounds


def contract_kernel(which, half, table, target, bounds, amps, fetched, out, acc):
    low, high = bounds[which], bounds[which + 1]
    acc[...] = jnp.zeros_like(acc)

    def step(i, carry):
        products = []
        for u in range(UNROLL):
            j = low + i * UNROLL + u
            codes = [table[j * PAIR + n] for n in range(PAIR)]
            left = jnp.concatenate([amps[c & 31] for c in codes], axis=1)
            right = jnp.concatenate([fetched[c >> 5] for c in codes], axis=0)
            products.append(jnp.dot(left, right, preferred_element_type=jnp.float32))
        for u in range(UNROLL):
            j = low + i * UNROLL + u
            tile = jnp.where(j < high, target[j] - which * half, half)
            acc[tile] += products[u]
        return carry

    lax.fori_loop(0, (high - low + UNROLL - 1) // UNROLL, step, 0)
    out[...] = acc[:half]


def contract(which, tables, amps, fetched, half):
    size = amps.shape[1]
    full = lambda n: pl.BlockSpec((n, size, size), lambda i, *_: (0, 0, 0))
    return pl.pallas_call(
        functools.partial(contract_kernel, which, half),
        grid_spec=pltpu.PrefetchScalarGridSpec(
            num_scalar_prefetch=3,
            grid=(1,),
            in_specs=[full(amps.shape[0]), full(fetched.shape[0])],
            out_specs=full(half),
            scratch_shapes=[pltpu.VMEM((half + 1, size, size), jnp.float32)],
        ),
        out_shape=jax.ShapeDtypeStruct((half, size, size), jnp.float32),
        compiler_params=pltpu.CompilerParams(vmem_limit_bytes=40 << 20),
        cost_estimate=pl.CostEstimate(
            flops=1 << 32, bytes_accessed=4 << 20, transcendentals=0
        ),
        name="contract_%d" % which,
    )(*tables, amps, fetched)


def encode_kernel(own, other, out):
    size = own.shape[1]
    for i in range(own.shape[0]):
        v = own[i] + other[i]
        top = jnp.max(jnp.abs(v), axis=0, keepdims=True)
        scale = jnp.ceil(jnp.log2(jnp.maximum(top, 1e-32)) * STEPS + 0.01)
        codes = v * (jnp.exp2(scale * (-1.0 / STEPS)) * TOP)
        out[i, :size] = jnp.floor(codes + 0.5).astype(jnp.int32).astype(jnp.int16)
        row = jnp.broadcast_to(scale, (out.shape[1] - size, size))
        out[i, size:] = row.astype(jnp.int32).astype(jnp.int16)


def encode(own, other, block=4):
    tiles, size, _ = own.shape
    spec = lambda rows: pl.BlockSpec((block, rows, size), lambda i: (i, 0, 0))
    return pl.pallas_call(
        encode_kernel,
        grid=(tiles // block,),
        in_specs=[spec(size), spec(size)],
        out_specs=spec(size + 16),
        out_shape=jax.ShapeDtypeStruct((tiles, size + 16, size), jnp.int16),
        cost_estimate=pl.CostEstimate(flops=1 << 20, bytes_accessed=3 << 20, transcendentals=0),
        name="encode",
    )(own, other)


def decode_kernel(pieces, out):
    size = out.shape[1]
    total = jnp.zeros((size, size), jnp.float32)
    for i in range(pieces.shape[0]):
        scale = pieces[i, size:].astype(jnp.int32).astype(jnp.float32)[:1]
        codes = pieces[i, :size].astype(jnp.int32).astype(jnp.float32)
        total += codes * (jnp.exp2(scale * (1.0 / STEPS)) * (1.0 / TOP))
    out[0] = total


def decode(pieces):
    size = pieces.shape[2]
    return pl.pallas_call(
        decode_kernel,
        out_shape=jax.ShapeDtypeStruct((1, size, size), jnp.float32),
        cost_estimate=pl.CostEstimate(flops=1 << 20, bytes_accessed=1 << 20, transcendentals=0),
        name="decode",
    )(pieces)


def per_device(amplitudes, integrals, tasks, requests, counts):
    tile = amplitudes.shape[1]
    half = lax.axis_size("z")
    wanted = lax.all_to_all(requests, "group", split_axis=0, concat_axis=0, tiled=True)
    fetched = lax.all_to_all(
        integrals[wanted], "group", split_axis=0, concat_axis=0, tiled=True
    ).reshape(-1, tile, tile)
    tables = task_tables(tasks, counts, lax.axis_index("core"), 2 * half)
    amps = jnp.concatenate([amplitudes, jnp.zeros((1, tile, tile), amplitudes.dtype)])
    other = contract(0, tables, amps, fetched, half)
    other = lax.ppermute(other, "core", [(0, 1), (1, 0)])
    own = contract(1, tables, amps, fetched, half)
    pieces = lax.all_to_all(encode(own, other), "z", split_axis=0, concat_axis=0, tiled=True)
    return decode(pieces)


def solution(mesh):
    finer = Mesh(mesh.devices.reshape(mesh.shape["group"], 16, 2), GROUP_MEMBER)
    placed = (
        P(GROUP_MEMBER, None, None),
        P(GROUP_MEMBER, None, None),
        P(GROUP_MEMBER, None),
        P(GROUP_MEMBER, None),
        P(GROUP_MEMBER),
    )
    return jax.shard_map(
        per_device,
        mesh=finer,
        in_specs=placed,
        out_specs=P(GROUP_MEMBER, None, None),
        check_vma=False,
    )
```

time: 360 us -> 117 us (0.33)
  the two profiles are of different devices: /device:TPU:6 before, /device:TPU:8 now
where the time goes in v1:
time: 117 us; the launch traced here: 116 us
  blocking collectives  56.4 us (48%)
  waiting for transfers between devices  25.4 us (22%)
  starting transfers between devices  16 us (14%)
  Pallas kernels  8.12 us (7%)
  local copies, waits for them, and re-layouts  6.52 us (6%)
  other arithmetic  3.03 us (3%)
    all_to_all x1, blocking collectives, per_device(): lax.all_to_all(encode(own, other), 'z', split_axis=0, concat_axis=0, tile...  56.4 us
    all_to_all x1, waiting for transfers between devices, per_device(): lax.all_to_all(integrals[wanted], 'group', split_axis=0, concat_axis=0, t...  21.4 us
    all_to_all x1, starting transfers between devices, per_device(): lax.all_to_all(requests, 'group', split_axis=0, concat_axis=0, tiled=True)  9.1 us
    all_to_all x1, starting transfers between devices, per_device(): lax.all_to_all(integrals[wanted], 'group', split_axis=0, concat_axis=0, t...  4.96 us
    pallas_call x1, Pallas kernels, encode(): pl.pallas_call(encode_kernel, grid=(tiles // block,), in_specs=[spec(size...  3.63 us
    all_to_all x1, waiting for transfers between devices, per_device(): lax.all_to_all(requests, 'group', split_axis=0, concat_axis=0, tiled=True)  3.58 us
    pallas_call x2, Pallas kernels, contract(): pl.pallas_call(functools.partial(contract_kernel, which, half), grid_spec...  2.65 us
  transfers between devices with their start and end apart: 3, of which 3 were waited for; matrix products, arithmetic and copies ran while one was open for 4% of the time, Pallas kernels for 1%

profile of v1, /device:TPU:8, one launch (start us, length us, event | category | flops | bytes accessed | tf_op | source)
XLA Modules:
  0.0 116.2 jit_solution(2533488695697932059)
XLA Ops:
  0.0 0.0 copy-start
  0.0 1.4 %copy.11 = s32[16,1,4]{2,1,0:T(1,128)} copy(s32[16,1,4]{0,2,1:T(4,128)} %bitcast.16) | data formatting | bytes 512 | tf_op jit(solution)/shard_map/all_to_all | solution.py:133
  1.4 9.1 %all-to-all-start = ((s32[16,1,4]{2,1,0:T(1,128)}), s32[16,1,4]{2,1,0:T(1,128)S(1)}, u32[]{:S(2)}, u32[]{:S(2)}) async-start(s32[16,1,4]{2,1,0:T(1,128)} %copy.11), calls=%async_computation | async-start | bytes 16384 | tf_op jit(solution)/shard_map/all_to_all | solution.py:133
  11.2 0.8 shift-right-arithmetic_add_fusion
  12.0 1.1 concatenate.3.amps
  13.1 3.6 %all-to-all-done = s32[16,1,4]{2,1,0:T(1,128)S(1)} async-done(((s32[16,1,4]{2,1,0:T(1,128)}), s32[16,1,4]{2,1,0:T(1,128)S(1)}, u32[]{:S(2)}, u32[]{:S(2)}) %all-to-all-start) | async-done | bytes 288 | tf_op jit(solution)/shard_map/all_to_all | solution.py:133
  16.7 0.1 copy.12
  16.8 0.1 copy.13
  16.9 0.1 reshape.138
  17.0 0.0 copy-done
  17.0 2.2 %gather_fusion = bf16[64,128,128]{2,1,0:T(8,128)(2,1)} fusion(bf16[8,128,128]{2,1,0:T(8,128)(2,1)S(1)} %copy-done, s32[1024]{0:T(1024)S(1)} %pad_clamp_fusion), kind=kCustom, calls=%fused_computation | custom fusion | bytes 4194560 | tf_op jit(solution)/shard_map/gather | solution.py:135
  19.1 5.0 %all-to-all-start.1 = ((bf16[16,4,128,128]{3,2,1,0:T(8,128)(2,1)}), bf16[16,4,128,128]{3,2,1,0:T(8,128)(2,1)S(1)}, u32[]{:S(2)}, u32[]{:S(2)}) async-start(bf16[16,4,128,128]{3,2,1,0:T(8,128)(2,1)} %bitcast.14), calls=%async_computation.1 | async-start | bytes 4194304 | tf_op jit(solution)/shard_map/all_to_all | solution.py:134
  24.1 0.1 convert_reduce_fusion.1
  24.2 0.1 select_reduce_fusion.2
  24.3 0.6 fusion.5
  25.0 1.3 %pad_add_fusion.bounds = s32[3]{0:T(128)S(1)} fusion(s32[1]{0:T(128)} %get-tuple-element.10, s32[1]{0:T(128)} %get-tuple-element.9, s32[1]{0:T(128)} %constant.41.clone.1), kind=kLoop, calls=%fused_computation.29 | loop fusion | flops 6 | bytes 24 | tf_op jit(solution)/shard_map/stack | solution.py:37
  26.3 0.1 convert_reduce_fusion.2.target
  26.4 0.1 select_reduce_fusion.1
  26.5 0.2 convert_reduce_fusion
  26.7 0.2 select_reduce_fusion
  26.9 21.4 %all-to-all-done.1 = bf16[16,4,128,128]{3,2,1,0:T(8,128)(2,1)S(1)} async-done(((bf16[16,4,128,128]{3,2,1,0:T(8,128)(2,1)}), bf16[16,4,128,128]{3,2,1,0:T(8,128)(2,1)S(1)}, u32[]{:S(2)}, u32[]{:S(2)}) %all-to-all-start.1) | async-done | bytes 2097184 | tf_op jit(solution)/shard_map/all_to_all | solution.py:134
  48.4 1.3 %contract_0.1 = f32[16,128,128]{2,1,0:T(8,128)S(1)} custom-call(s32[512]{0:T(512)S(1)} %broadcast_add_fusion.table, s32[256]{0:T(256)S(1)} %convert_reduce_fusion.2.target, s32[3]{0:T(128)S(1)} %pad_add_fusion.bounds, bf16[17,128,128]{2,1,0:T(8,128)(2,1)S(1)} %concatenate.3.amps, bf16[64,128,128]{2,1,0:T(8,128)(2,1)S(1)} %bitcast.12), custom_call_target="tpu_custom_call" | custom-call | flops 4294967296 | bytes 4194304 | tf_op jit(solution)/shard_map/contract_0/pallas_call | solution.py:66
  49.7 1.9 %collective-permute-start = (f32[16,128,128]{2,1,0:T(8,128)S(1)}, f32[16,128,128]{2,1,0:T(8,128)}, u32[]{:S(2)}, u32[]{:S(2)}) collective-permute-start(f32[16,128,128]{2,1,0:T(8,128)S(1)} %contract_0.1), channel_id=1, source_target_pairs={{0,1},{1,0},{2,3},{3,2},{4,5},{5,4},{6,7},{7,6},{8,9},{9,8},{10,11... | collective-permute-start | bytes 3145736 | tf_op jit(solution)/shard_map/ppermute | solution.py:140
  51.6 1.3 %contract_1.1.own = f32[16,128,128]{2,1,0:T(8,128)S(1)} custom-call(s32[512]{0:T(512)S(1)} %broadcast_add_fusion.table, s32[256]{0:T(256)S(1)} %convert_reduce_fusion.2.target, s32[3]{0:T(128)S(1)} %pad_add_fusion.bounds, bf16[17,128,128]{2,1,0:T(8,128)(2,1)S(1)} %concatenate.3.amps, bf16[64,128,128]{2,1,0:T(8,128)(2,1)S(1)} %bitcast.13), custom_call_target="tpu_custom_call" | custom-call | flops 4294967296 | bytes 4194304 | tf_op jit(solution)/shard_map/contract_1/pallas_call | solution.py:66
  52.9 0.0 copy-start.1
  53.0 1.0 copy-done.1
  53.9 0.4 collective-permute-done.other
  54.4 3.6 %encode.1 = s16[16,144,128]{2,1,0:T(8,128)(2,1)} custom-call(f32[16,128,128]{2,1,0:T(8,128)} %copy-done.1, f32[16,128,128]{2,1,0:T(8,128)} %collective-permute-done.other), custom_call_target="tpu_custom_call" | custom-call | flops 1048576 | bytes 3145728 | tf_op jit(solution)/shard_map/encode/pallas_call | solution.py:99
  58.0 56.4 %all_to_all.22.pieces = s16[16,144,128]{2,1,0:T(8,128)(2,1)} all-to-all(s16[16,144,128]{2,1,0:T(8,128)(2,1)} %encode.1), channel_id=1, replica_groups=mesh['group'=16,'z'=16,'core'=2] {'z'}, dimensions={0} | all-to-all | bytes 1179648 | tf_op jit(solution)/shard_map/all_to_all | solution.py:142
  114.4 1.8 %decode.1 = f32[1,128,128]{2,1,0:T(8,128)} custom-call(s16[16,144,128]{2,1,0:T(8,128)(2,1)} %all_to_all.22.pieces), custom_call_target="tpu_custom_call" | custom-call | flops 1048576 | bytes 1048576 | tf_op jit(solution)/shard_map/decode/pallas_call | solution.py:122
  (8 shorter events, 0.1 us)
Async XLA Ops:
  0.0 17.0 %copy-start = (bf16[8,128,128]{2,1,0:T(8,128)(2,1)S(1)}, bf16[8,128,128]{2,1,0:T(8,128)(2,1)}, u32[]{:S(2)}) copy-start(bf16[8,128,128]{2,1,0:T(8,128)(2,1)} %param.6) | copy-start | bytes 786436
  1.4 15.3 %all-to-all-start = ((s32[16,1,4]{2,1,0:T(1,128)}), s32[16,1,4]{2,1,0:T(1,128)S(1)}, u32[]{:S(2)}, u32[]{:S(2)}) async-start(s32[16,1,4]{2,1,0:T(1,128)} %copy.11), calls=%async_computation | async-start | bytes 16384 | tf_op jit(solution)/shard_map/all_to_all | solution.py:133
  19.1 29.2 %all-to-all-start.1 = ((bf16[16,4,128,128]{3,2,1,0:T(8,128)(2,1)}), bf16[16,4,128,128]{3,2,1,0:T(8,128)(2,1)S(1)}, u32[]{:S(2)}, u32[]{:S(2)}) async-start(bf16[16,4,128,128]{3,2,1,0:T(8,128)(2,1)} %bitcast.14), calls=%async_computation.1 | async-start | bytes 4194304 | tf_op jit(solution)/shard_map/all_to_all | solution.py:134
  49.7 4.7 %collective-permute-start = (f32[16,128,128]{2,1,0:T(8,128)S(1)}, f32[16,128,128]{2,1,0:T(8,128)}, u32[]{:S(2)}, u32[]{:S(2)}) collective-permute-start(f32[16,128,128]{2,1,0:T(8,128)S(1)} %contract_0.1), channel_id=1, source_target_pairs={{0,1},{1,0},{2,3},{3,2},{4,5},{5,4},{6,7},{7,6},{8,9},{9,8},{10,11... | collective-permute-start | bytes 3145736 | tf_op jit(solution)/shard_map/ppermute | solution.py:140
  52.9 1.0 copy-start.1

commit v2 on v1

--- a/solution.py
+++ b/solution.py
@@ -14,6 +14,29 @@
 SLOTS = 512
 TOP = 32760.0
 STEPS = 128.0
+
+
+def select_kernel(wanted, tiles, out):
+    for i in range(out.shape[0]):
+        out[i] = tiles[wanted[i]]
+
+
+def select(wanted, tiles):
+    size = tiles.shape[1]
+    full = lambda n: pl.BlockSpec((n, size, size), lambda i, *_: (0, 0, 0))
+    return pl.pallas_call(
+        select_kernel,
+        grid_spec=pltpu.PrefetchScalarGridSpec(
+            num_scalar_prefetch=1,
+            grid=(1,),
+            in_specs=[full(tiles.shape[0])],
+            out_specs=full(wanted.shape[0]),
+        ),
+        out_shape=jax.ShapeDtypeStruct((wanted.shape[0], size, size), tiles.dtype),
+        compiler_params=pltpu.CompilerParams(vmem_limit_bytes=16 << 20),
+        cost_estimate=pl.CostEstimate(flops=0, bytes_accessed=2 << 20, transcendentals=0),
+        name="select",
+    )(wanted, tiles)
 
 
 def task_tables(tasks, counts, core, tiles):
@@ -73,7 +96,7 @@
             scratch_shapes=[pltpu.VMEM((half + 1, size, size), jnp.float32)],
         ),
         out_shape=jax.ShapeDtypeStruct((half, size, size), jnp.float32),
-        compiler_params=pltpu.CompilerParams(vmem_limit_bytes=40 << 20),
+        compiler_params=pltpu.CompilerParams(vmem_limit_bytes=16 << 20),
         cost_estimate=pl.CostEstimate(
             flops=1 << 32, bytes_accessed=4 << 20, transcendentals=0
         ),
@@ -93,15 +116,12 @@
         out[i, size:] = row.astype(jnp.int32).astype(jnp.int16)
 
 
-def encode(own, other, block=4):
+def encode(own, other):
     tiles, size, _ = own.shape
-    spec = lambda rows: pl.BlockSpec((block, rows, size), lambda i: (i, 0, 0))
     return pl.pallas_call(
         encode_kernel,
-        grid=(tiles // block,),
-        in_specs=[spec(size), spec(size)],
-        out_specs=spec(size + 16),
         out_shape=jax.ShapeDtypeStruct((tiles, size + 16, size), jnp.int16),
+        compiler_params=pltpu.CompilerParams(vmem_limit_bytes=16 << 20),
         cost_estimate=pl.CostEstimate(flops=1 << 20, bytes_accessed=3 << 20, transcendentals=0),
         name="encode",
     )(own, other)
@@ -122,6 +142,7 @@
     return pl.pallas_call(
         decode_kernel,
         out_shape=jax.ShapeDtypeStruct((1, size, size), jnp.float32),
+        compiler_params=pltpu.CompilerParams(vmem_limit_bytes=4 << 20),
         cost_estimate=pl.CostEstimate(flops=1 << 20, bytes_accessed=1 << 20, transcendentals=0),
         name="decode",
     )(pieces)
@@ -130,12 +151,14 @@
 def per_device(amplitudes, integrals, tasks, requests, counts):
     tile = amplitudes.shape[1]
     half = lax.axis_size("z")
-    wanted = lax.all_to_all(requests, "group", split_axis=0, concat_axis=0, tiled=True)
-    fetched = lax.all_to_all(
-        integrals[wanted], "group", split_axis=0, concat_axis=0, tiled=True
-    ).reshape(-1, tile, tile)
+    asked = jnp.clip(requests, 0, integrals.shape[0] - 1)
+    wanted = lax.all_to_all(asked, "group", split_axis=0, concat_axis=0, tiled=True).reshape(-1)
     tables = task_tables(tasks, counts, lax.axis_index("core"), 2 * half)
     amps = jnp.concatenate([amplitudes, jnp.zeros((1, tile, tile), amplitudes.dtype)])
+    wanted, tables, amps = lax.optimization_barrier((wanted, tables, amps))
+    fetched = lax.all_to_all(
+        select(wanted, integrals), "group", split_axis=0, concat_axis=0, tiled=True
+    )
     other = contract(0, tables, amps, fetched, half)
     other = lax.ppermute(other, "core", [(0, 1), (1, 0)])
     own = contract(1, tables, amps, fetched, half)

time: 117 us -> 113 us (0.966)
  the two profiles are of different devices: /device:TPU:8 before, /device:TPU:1 now
where the time goes in v2:
time: 113 us; the launch traced here: 112 us
  blocking collectives  81.2 us (72%)
  starting transfers between devices  12.9 us (11%)
  Pallas kernels  8.17 us (7%)
  other arithmetic  4.31 us (4%)
  local copies, waits for them, and re-layouts  3.93 us (3%)
    all_to_all x1, blocking collectives, per_device(): lax.all_to_all(encode(own, other), 'z', split_axis=0, concat_axis=0, tile...  50.7 us
    all_to_all x1, blocking collectives, per_device(): lax.all_to_all(select(wanted, integrals), 'group', split_axis=0, concat_a...  30.5 us
    all_to_all x1, starting transfers between devices, per_device(): lax.all_to_all(asked, 'group', split_axis=0, concat_axis=0, tiled=True)  7.58 us
    pallas_call x2, Pallas kernels, contract(): pl.pallas_call(functools.partial(contract_kernel, which, half), grid_spec...  6.36 us
    ppermute x1, starting transfers between devices, per_device(): other = lax.ppermute(other, 'core', [(0, 1), (1, 0)])  5.36 us
  transfers between devices with their start and end apart: 2, of which 1 were waited for; matrix products, arithmetic and copies ran while one was open for 4% of the time, Pallas kernels for 3%

profile of v2, /device:TPU:1, one launch (start us, length us, event | category | flops | bytes accessed | tf_op | source)
XLA Modules:
  0.0 112.3 jit_solution(581101579989858653)
XLA Ops:
  0.0 0.7 clamp_bitcast_fusion
  0.7 0.7 copy.9
  1.4 7.6 %all-to-all-start = ((s32[16,1,4]{2,1,0:T(1,128)}), s32[16,1,4]{2,1,0:T(1,128)S(1)}, u32[]{:S(2)}, u32[]{:S(2)}) async-start(s32[16,1,4]{2,1,0:T(1,128)} %copy.9), calls=%async_computation | async-start | bytes 16384 | tf_op jit(solution)/shard_map/all_to_all | solution.py:155
  9.6 0.8 shift-right-arithmetic_add_fusion
  10.5 0.1 convert_reduce_fusion.1
  10.6 0.1 select_reduce_fusion.2
  10.7 0.1 convert_reduce_fusion.2.target
  10.8 0.6 fusion.5
  11.4 0.2 convert_reduce_fusion
  11.6 0.1 select_reduce_fusion.1
  11.7 0.2 select_reduce_fusion
  11.9 1.3 %pad_add_fusion.bounds = s32[3]{0:T(128)S(1)} fusion(s32[1]{0:T(128)} %get-tuple-element.20, s32[1]{0:T(128)} %get-tuple-element.19, s32[1]{0:T(128)} %constant.41.clone.1), kind=kLoop, calls=%fused_computation.27 | loop fusion | flops 6 | bytes 24 | tf_op jit(solution)/shard_map/stack | solution.py:60
  13.2 1.1 concatenate.3.amps
  14.3 1.0 all-to-all-done
  15.3 0.5 broadcast.169
  15.8 0.7 reduce.8
  16.5 0.1 reshape.107.wanted
  16.6 0.0 copy-start
  16.6 0.9 copy-done
  17.5 0.7 select.32
  18.2 30.5 %all_to_all.19.fetched = bf16[64,128,128]{2,1,0:T(8,128)(2,1)S(1)} all-to-all(bf16[64,128,128]{2,1,0:T(8,128)(2,1)S(1)} %select.32), channel_id=1, replica_groups=mesh['group'=16,'z'=16,'core'=2] {'group'}, dimensions={0} | all-to-all | bytes 4194304 | tf_op jit(solution)/shard_map/all_to_all | solution.py:159
  48.7 3.2 %contract_0.1 = f32[16,128,128]{2,1,0:T(8,128)S(1)} custom-call(s32[512]{0:T(512)S(1)} %broadcast_add_fusion.table, s32[256]{0:T(256)S(1)} %convert_reduce_fusion.2.target, s32[3]{0:T(128)S(1)} %pad_add_fusion.bounds, bf16[17,128,128]{2,1,0:T(8,128)(2,1)S(1)} %concatenate.3.amps, bf16[64,128,128]{2,1,0:T(8,128)(2,1)S(1)} %all_to_all.19.fetched), custom_call_target="tpu_custom_call" | custom-call | flops 4294967296 | bytes 4194304 | tf_op jit(solution)/shard_map/contract_0/pallas_call | solution.py:89
  51.9 5.4 %collective-permute-start = (f32[16,128,128]{2,1,0:T(8,128)S(1)}, f32[16,128,128]{2,1,0:T(8,128)S(1)}, u32[]{:S(2)}, u32[]{:S(2)}) collective-permute-start(f32[16,128,128]{2,1,0:T(8,128)S(1)} %contract_0.1), channel_id=1, source_target_pairs={{0,1},{1,0},{2,3},{3,2},{4,5},{5,4},{6,7},{7,6},{8,9},{9,8},{10,11... | collective-permute-start | bytes 3145736 | tf_op jit(solution)/shard_map/ppermute | solution.py:163
  57.2 3.2 %contract_1.1.own = f32[16,128,128]{2,1,0:T(8,128)S(1)} custom-call(s32[512]{0:T(512)S(1)} %broadcast_add_fusion.table, s32[256]{0:T(256)S(1)} %convert_reduce_fusion.2.target, s32[3]{0:T(128)S(1)} %pad_add_fusion.bounds, bf16[17,128,128]{2,1,0:T(8,128)(2,1)S(1)} %concatenate.3.amps, bf16[64,128,128]{2,1,0:T(8,128)(2,1)S(1)} %all_to_all.19.fetched), custom_call_target="tpu_custom_call" | custom-call | flops 4294967296 | bytes 4194304 | tf_op jit(solution)/shard_map/contract_1/pallas_call | solution.py:89
  60.4 0.0 collective-permute-done.other
  60.4 0.4 encode.1
  60.8 50.7 %all_to_all.20.pieces = s16[16,144,128]{2,1,0:T(8,128)(2,1)S(1)} all-to-all(s16[16,144,128]{2,1,0:T(8,128)(2,1)S(1)} %encode.1), channel_id=1, replica_groups=mesh['group'=16,'z'=16,'core'=2] {'z'}, dimensions={0} | all-to-all | bytes 1179648 | tf_op jit(solution)/shard_map/all_to_all | solution.py:165
  111.5 0.8 decode.1
  (6 shorter events, 0.1 us)
Async XLA Ops:
  1.4 13.9 %all-to-all-start = ((s32[16,1,4]{2,1,0:T(1,128)}), s32[16,1,4]{2,1,0:T(1,128)S(1)}, u32[]{:S(2)}, u32[]{:S(2)}) async-start(s32[16,1,4]{2,1,0:T(1,128)} %copy.9), calls=%async_computation | async-start | bytes 16384 | tf_op jit(solution)/shard_map/all_to_all | solution.py:155
  16.6 1.0 copy-start
  51.9 8.6 %collective-permute-start = (f32[16,128,128]{2,1,0:T(8,128)S(1)}, f32[16,128,128]{2,1,0:T(8,128)S(1)}, u32[]{:S(2)}, u32[]{:S(2)}) collective-permute-start(f32[16,128,128]{2,1,0:T(8,128)S(1)} %contract_0.1), channel_id=1, source_target_pairs={{0,1},{1,0},{2,3},{3,2},{4,5},{5,4},{6,7},{7,6},{8,9},{9,8},{10,11... | collective-permute-start | bytes 3145736 | tf_op jit(solution)/shard_map/ppermute | solution.py:163

commit v3 on v2

v3 whole, which is shorter than its diff:
```python
import functools

import jax
import jax.numpy as jnp
from jax import lax
from jax.experimental import pallas as pl
from jax.experimental.pallas import tpu as pltpu
from jax.sharding import Mesh
from jax.sharding import PartitionSpec as P

GROUP_MEMBER = ("group", "zh", "zl", "core")
Z = ("zh", "zl")
PAIR = 2
UNROLL = 8
SLOTS = 512
TOP = 32760.0
SCALE_ROWS = 8
STEPS = 128.0


def select_kernel(base, wanted, local, out):
    rows, _, cap = wanted.shape
    for i in range(rows):
        for c in range(cap):
            out[i * cap + c] = local[base + wanted[i, 0, c]]


def select(wanted, local, base):
    size = local.shape[1]
    slots = wanted.shape[0] * wanted.shape[2]
    full = lambda n: pl.BlockSpec((n, size, size), lambda i, *_: (0, 0, 0))
    return pl.pallas_call(
        functools.partial(select_kernel, base),
        grid_spec=pltpu.PrefetchScalarGridSpec(
            num_scalar_prefetch=1,
            grid=(1,),
            in_specs=[full(local.shape[0])],
            out_specs=full(slots),
        ),
        out_shape=jax.ShapeDtypeStruct((slots, size, size), local.dtype),
        compiler_params=pltpu.CompilerParams(vmem_limit_bytes=16 << 20),
        cost_estimate=pl.CostEstimate(flops=0, bytes_accessed=2 << 20, transcendentals=0),
        name="select",
    )(wanted, local)


def task_tables(tasks, counts, core, parity, tiles, blank):
    a, s, r = tasks.T
    half = tiles // 2
    k = jnp.arange(tasks.shape[0], dtype=jnp.int32)
    valid = k < counts[0]
    side = ((r & 1) ^ core ^ 1) * half + (((r >> 1) & 1) ^ parity ^ 1) * (half // 2) + (r >> 2)
    q = jnp.where(valid, side, tiles)
    code = a + s * 32
    rank = jnp.sum(((q[:, None] == q[None, :]) & (k[None, :] < k[:, None])).astype(jnp.int32), 1)
    b = jnp.arange(tiles, dtype=jnp.int32)
    hot = q[:, None] == b[None, :]
    groups = (jnp.sum(hot.astype(jnp.int32), 0) + PAIR - 1) // PAIR
    ends = jnp.sum(jnp.where(b[:, None] <= b[None, :], groups[:, None], 0), 0)
    first = jnp.sum(jnp.where(hot, (ends - groups)[None, :], 0), 1)
    place = jnp.where(valid, first * PAIR + rank, -1)
    p = jnp.arange(SLOTS, dtype=jnp.int32)
    table = blank + jnp.sum(jnp.where(place[:, None] == p[None, :], code[:, None] - blank, 0), 0)
    j = jnp.arange(SLOTS // PAIR, dtype=jnp.int32)
    target = jnp.sum((ends[:, None] <= j[None, :]).astype(jnp.int32), 0)
    return table, target, ends


def contract_kernel(which, half, table, target, ends, amps, fetched, out, acc):
    low = ends[half - 1] if which else 0
    high = ends[which * half + half - 1]
    acc[...] = jnp.zeros_like(acc)

    def step(i, carry):
        products = []
        for u in range(UNROLL):
            j = low + i * UNROLL + u
            codes = [table[j * PAIR + n] for n in range(PAIR)]
            left = jnp.concatenate([amps[c & 31] for c in codes], axis=1)
            right = jnp.concatenate([fetched[c >> 5] for c in codes], axis=0)
            products.append(jnp.dot(left, right, preferred_element_type=jnp.float32))
        for u in range(UNROLL):
            j = low + i * UNROLL + u
            tile = jnp.where(j < high, target[j] - which * half, half)
            acc[tile] += products[u]
        return carry

    lax.fori_loop(0, (high - low + UNROLL - 1) // UNROLL, step, 0)
    out[...] = acc[:half]


def contract(which, tables, amps, fetched, half):
    size = amps.shape[1]
    full = lambda n: pl.BlockSpec((n, size, size), lambda i, *_: (0, 0, 0))
    return pl.pallas_call(
        functools.partial(contract_kernel, which, half),
        grid_spec=pltpu.PrefetchScalarGridSpec(
            num_scalar_prefetch=3,
            grid=(1,),
            in_specs=[full(amps.shape[0]), full(fetched.shape[0])],
            out_specs=full(half),
            scratch_shapes=[pltpu.VMEM((half + 1, size, size), jnp.float32)],
        ),
        out_shape=jax.ShapeDtypeStruct((half, size, size), jnp.float32),
        compiler_params=pltpu.CompilerParams(vmem_limit_bytes=16 << 20),
        cost_estimate=pl.CostEstimate(
            flops=1 << 32, bytes_accessed=4 << 20, transcendentals=0
        ),
        name="contract_%d" % which,
    )(*tables, amps, fetched)


def store_coded(v, out, i):
    rows = v.shape[0]
    top = jnp.max(jnp.abs(v), axis=0, keepdims=True)
    scale = jnp.ceil(jnp.log2(jnp.maximum(top, 1e-32)) * STEPS + 0.01)
    codes = v * (jnp.exp2(scale * (-1.0 / STEPS)) * TOP)
    out[i, :rows] = jnp.floor(codes + 0.5).astype(jnp.int32).astype(jnp.int16)
    row = jnp.broadcast_to(scale, (SCALE_ROWS, v.shape[1]))
    out[i, rows:] = row.astype(jnp.int32).astype(jnp.int16)


def load_coded(coded, i):
    rows = coded.shape[1] - SCALE_ROWS
    scale = coded[i, rows:].astype(jnp.int32).astype(jnp.float32)[:1]
    codes = coded[i, :rows].astype(jnp.int32).astype(jnp.float32)
    return codes * (jnp.exp2(scale * (1.0 / STEPS)) * (1.0 / TOP))


def plain_call(kernel, name, outs, *args):
    return pl.pallas_call(
        kernel,
        out_shape=outs,
        compiler_params=pltpu.CompilerParams(vmem_limit_bytes=8 << 20),
        cost_estimate=pl.CostEstimate(flops=1 << 20, bytes_accessed=2 << 20, transcendentals=0),
        name=name,
    )(*args)


def give_kernel(own, other, upper, lower):
    mid = own.shape[1] // 2
    for i in range(upper.shape[0]):
        store_coded(own[i, :mid] + other[i, :mid], upper, i)
        store_coded(own[i, mid:] + other[i, mid:], lower, i)


def take_kernel(own, other, upper, lower, out):
    for i in range(upper.shape[0]):
        k = upper.shape[0] + i
        more = jnp.concatenate([load_coded(upper, i), load_coded(lower, i)], axis=0)
        store_coded(own[k] + other[k] + more, out, i)


def finish_kernel(pieces, out):
    total = load_coded(pieces, 0)
    for i in range(1, pieces.shape[0]):
        total += load_coded(pieces, i)
    out[0] = total


def reduce_members(own, other):
    tiles, size, _ = own.shape
    coded = lambda rows: jax.ShapeDtypeStruct((tiles // 2, rows + SCALE_ROWS, size), jnp.int16)
    upper, lower = plain_call(give_kernel, "give", [coded(size // 2)] * 2, own, other)
    upper = lax.ppermute(upper, Z, [(z, z ^ 1) for z in range(tiles)])
    lower = lax.ppermute(lower, Z, [(z, (z + 1 if z % 2 else z - 1) % tiles) for z in range(tiles)])
    pieces = plain_call(take_kernel, "take", coded(size), own, other, upper, lower)
    pieces = lax.all_to_all(pieces, "zh", split_axis=0, concat_axis=0, tiled=True)
    return plain_call(
        finish_kernel, "finish", jax.ShapeDtypeStruct((1, size, size), jnp.float32), pieces
    )


def per_device(amplitudes, integrals, tasks, requests, counts):
    amount, tile, _ = amplitudes.shape
    half = lax.axis_size(Z)
    asked = requests.reshape(requests.shape[0], 1, requests.shape[1])
    wanted = lax.all_to_all(asked, "group", split_axis=0, concat_axis=0, tiled=True)
    core, parity = lax.axis_index("core"), lax.axis_index("zl")
    tables = task_tables(tasks, counts, core, parity, 2 * half, amount)
    blank = jnp.zeros((1, tile, tile), amplitudes.dtype)
    local = jnp.concatenate([amplitudes, blank, integrals])
    wanted, tables, local = lax.optimization_barrier((wanted, tables, local))
    fetched = lax.all_to_all(
        select(wanted, local, amount + 1), "group", split_axis=0, concat_axis=0, tiled=True
    )
    other = contract(0, tables, local, fetched, half)
    other = lax.ppermute(other, "core", [(0, 1), (1, 0)])
    own = contract(1, tables, local, fetched, half)
    return reduce_members(own, other)


def solution(mesh):
    finer = Mesh(mesh.devices.reshape(mesh.shape["group"], 8, 2, 2), GROUP_MEMBER)
    placed = (
        P(GROUP_MEMBER, None, None),
        P(GROUP_MEMBER, None, None),
        P(GROUP_MEMBER, None),
        P(GROUP_MEMBER, None),
        P(GROUP_MEMBER),
    )
    return jax.shard_map(
        per_device,
        mesh=finer,
        in_specs=placed,
        out_specs=P(GROUP_MEMBER, None, None),
        check_vma=False,
    )
```

time: 113 us -> 106 us (0.938)
  blocking collectives: 81.2 us -> 60 us
  starting transfers between devices: 12.9 us -> 29.8 us
  waiting for transfers between devices: 0.99 us -> 5.74 us
  Pallas kernels: 8.17 us -> 4.95 us
  local copies, waits for them, and re-layouts: 3.93 us -> 1.43 us
  other arithmetic: 4.31 us -> 2.95 us
    all_to_all x2, blocking collectives: 81.2 us -> 60 us  [the longest x1 31.2 us: reduce_members(): lax.all_to_all(pieces, 'zh', split_axis=0, concat_axis=0, tiled=True)]
    ppermute x0 -> x2, starting transfers between devices: none -> 13.5 us  [the longest x1 9.15 us: reduce_members(): lax.ppermute(lower, Z, [(z, (z + 1 if z % 2 else z - 1) % tiles) for z in...]
    pallas_call x2, Pallas kernels: 6.36 us -> 2.98 us  [contract(): pl.pallas_call(functools.partial(contract_kernel, which, half), grid_spec...]
    ppermute x1, starting transfers between devices: 5.36 us -> 8.74 us  [per_device(): other = lax.ppermute(other, 'core', [(0, 1), (1, 0)])]
    ppermute x0 -> x2, waiting for transfers between devices: none -> 2.51 us  [the longest x1 2.51 us: reduce_members(): lax.ppermute(lower, Z, [(z, (z + 1 if z % 2 else z - 1) % tiles) for z in...]
    all_to_all x1, waiting for transfers between devices: 0.98 us -> 2.62 us  [per_device(): lax.all_to_all(asked, 'group', split_axis=0, concat_axis=0, tiled=True)]
    all_to_all x2 -> x0, other arithmetic: 1.35 us -> none  [per_device(): lax.all_to_all(asked, 'group', split_axis=0, concat_axis=0, tiled=True)]
    reshape x1, local copies, waits for them, and re-layouts: 0.08 us -> 1.35 us  [per_device(): asked = requests.reshape(requests.shape[0], 1, requests.shape[1])]
  transfers between devices with their start and end apart: 2 -> 4, of which waited for: 1 -> 3; matrix products, arithmetic and copies ran while one was open for 4% -> 3% of each run, Pallas kernels for 3% -> 2%
where the time goes in v3:
time: 106 us
  blocking collectives  60 us (57%)
  starting transfers between devices  29.8 us (28%)
  waiting for transfers between devices  5.74 us (5%)
  Pallas kernels  4.95 us (5%)
  other arithmetic  2.95 us (3%)
  local copies, waits for them, and re-layouts  1.43 us (1%)
    all_to_all x1, blocking collectives, reduce_members(): lax.all_to_all(pieces, 'zh', split_axis=0, concat_axis=0, tiled=True)  31.2 us
    all_to_all x1, blocking collectives, per_device(): lax.all_to_all(select(wanted, local, amount + 1), 'group', split_axis=0,...  28.8 us
    ppermute x1, starting transfers between devices, reduce_members(): lax.ppermute(lower, Z, [(z, (z + 1 if z % 2 else z - 1) % tiles) for z in...  9.15 us
    ppermute x1, starting transfers between devices, per_device(): other = lax.ppermute(other, 'core', [(0, 1), (1, 0)])  8.74 us
    all_to_all x1, starting transfers between devices, per_device(): lax.all_to_all(asked, 'group', split_axis=0, concat_axis=0, tiled=True)  7.58 us
    ppermute x1, starting transfers between devices, reduce_members(): upper = lax.ppermute(upper, Z, [(z, z ^ 1) for z in range(tiles)])  4.36 us
    pallas_call x2, Pallas kernels, contract(): pl.pallas_call(functools.partial(contract_kernel, which, half), grid_spec...  2.98 us
    all_to_all x1, waiting for transfers between devices, per_device(): lax.all_to_all(asked, 'group', split_axis=0, concat_axis=0, tiled=True)  2.62 us
  transfers between devices with their start and end apart: 4, of which 3 were waited for; matrix products, arithmetic and copies ran while one was open for 3% of the time, Pallas kernels for 2%

profile of v3, /device:TPU:1, one launch (start us, length us, event | category | flops | bytes accessed | tf_op | source)
XLA Modules:
  0.0 105.7 jit_solution(9747634771206090307)
XLA Ops:
  0.0 1.4 %copy.7 = s32[16,1,4]{2,1,0:T(1,128)} copy(s32[16,1,4]{0,2,1:T(4,128)} %bitcast.8) | data formatting | bytes 512 | tf_op jit(solution)/shard_map/reshape | solution.py:177
  1.4 7.6 %all-to-all-start = ((s32[16,1,4]{2,1,0:T(1,128)}), s32[16,1,4]{2,1,0:T(1,128)S(1)}, u32[]{:S(2)}, u32[]{:S(2)}) async-start(s32[16,1,4]{2,1,0:T(1,128)} %copy.7), calls=%async_computation | async-start | bytes 16384 | tf_op jit(solution)/shard_map/all_to_all | solution.py:178
  9.6 0.8 add_add_fusion
  10.5 0.1 convert_reduce_fusion.1
  10.6 0.2 convert_reduce_fusion
  10.8 0.1 select_reduce_fusion.2.ends
  10.9 0.1 select_reduce_fusion.1
  11.0 0.2 select_reduce_fusion
  11.2 0.1 pad.1.clone
  11.3 1.3 %pad_maximum_fusion.local.amps = bf16[25,128,128]{2,1,0:T(8,128)(2,1)S(1)} fusion(bf16[8,128,128]{2,1,0:T(8,128)(2,1)} %param.6, bf16[16,128,128]{2,1,0:T(8,128)(2,1)} %param.5, bf16[25]{0:T(256)(128)(2,1)S(1)} %pad.1.clone), kind=kLoop, calls=%fused_computation | loop fusion | flops 819200 | bytes 1605682 | tf_op jit(solution)/shard_map/concatenate | solution.py:182
  12.6 0.1 convert_reduce_fusion.2.target
  12.7 2.6 %all-to-all-done.wanted = s32[16,1,4]{2,1,0:T(1,128)S(1)} async-done(((s32[16,1,4]{2,1,0:T(1,128)}), s32[16,1,4]{2,1,0:T(1,128)S(1)}, u32[]{:S(2)}, u32[]{:S(2)}) %all-to-all-start) | async-done | bytes 288 | tf_op jit(solution)/shard_map/all_to_all | solution.py:178
  15.3 0.8 select.31
  16.1 28.8 %all_to_all.15.fetched = bf16[64,128,128]{2,1,0:T(8,128)(2,1)S(1)} all-to-all(bf16[64,128,128]{2,1,0:T(8,128)(2,1)S(1)} %select.31), channel_id=1, replica_groups=mesh['group'=16,'zh'=8,'zl'=2,'core'=2] {'group'}, dimensions={0} | all-to-all | bytes 4194304 | tf_op jit(solution)/shard_map/all_to_all | solution.py:184
  44.9 1.3 %contract_0.1 = f32[16,128,128]{2,1,0:T(8,128)S(1)} custom-call(s32[512]{0:T(512)S(1)} %broadcast_add_fusion.table, s32[256]{0:T(256)S(1)} %convert_reduce_fusion.2.target, s32[32]{0:T(128)S(1)} %select_reduce_fusion.2.ends, bf16[25,128,128]{2,1,0:T(8,128)(2,1)S(1)} %pad_maximum_fusion.local.amps, bf16[64,128,128]{2,1,0:T(8,128)(2,1)S(1)} %all_to_all.15.fetched), custom_call_target="tpu_custom_call" | custom-call | flops 4294967296 | bytes 4194304 | tf_op jit(solution)/shard_map/contract_0/pallas_call | solution.py:95
  46.3 8.7 %collective-permute-start = (f32[16,128,128]{2,1,0:T(8,128)S(1)}, f32[16,128,128]{2,1,0:T(8,128)S(1)}, u32[]{:S(2)}, u32[]{:S(2)}) collective-permute-start(f32[16,128,128]{2,1,0:T(8,128)S(1)} %contract_0.1), channel_id=1, source_target_pairs={{0,1},{1,0},{2,3},{3,2},{4,5},{5,4},{6,7},{7,6},{8,9},{9,8},{10,11... | collective-permute-start | bytes 3145736 | tf_op jit(solution)/shard_map/ppermute | solution.py:188
  55.0 1.6 %contract_1.1.own = f32[16,128,128]{2,1,0:T(8,128)S(1)} custom-call(s32[512]{0:T(512)S(1)} %broadcast_add_fusion.table, s32[256]{0:T(256)S(1)} %convert_reduce_fusion.2.target, s32[32]{0:T(128)S(1)} %select_reduce_fusion.2.ends, bf16[25,128,128]{2,1,0:T(8,128)(2,1)S(1)} %pad_maximum_fusion.local.amps, bf16[64,128,128]{2,1,0:T(8,128)(2,1)S(1)} %all_to_all.15.fetched), custom_call_target="tpu_custom_call" | custom-call | flops 4294967296 | bytes 4194304 | tf_op jit(solution)/shard_map/contract_1/pallas_call | solution.py:95
  56.7 0.6 collective-permute-done.other
  57.3 0.2 give.1
  57.5 4.4 %collective-permute-start.1 = (s16[8,72,128]{2,1,0:T(8,128)(2,1)S(1)}, s16[8,72,128]{2,1,0:T(8,128)(2,1)S(1)}, u32[]{:S(2)}, u32[]{:S(2)}) collective-permute-start(s16[8,72,128]{2,1,0:T(8,128)(2,1)S(1)} %get-tuple-element.17), channel_id=1, source_target_pairs={{0,2},{2,0},{4,6},{6,4},{8,10},{10,8},{12,14},{14,12},{16,18},{18,... | collective-permute-start | bytes 442376 | tf_op jit(solution)/shard_map/ppermute | solution.py:165
  61.9 9.1 %collective-permute-start.2 = (s16[8,72,128]{2,1,0:T(8,128)(2,1)S(1)}, s16[8,72,128]{2,1,0:T(8,128)(2,1)S(1)}, u32[]{:S(2)}, u32[]{:S(2)}) collective-permute-start(s16[8,72,128]{2,1,0:T(8,128)(2,1)S(1)} %get-tuple-element.18), channel_id=1, source_target_pairs={{0,30},{2,4},{4,2},{6,8},{8,6},{10,12},{12,10},{14,16},{16,14},{18... | collective-permute-start | bytes 442376 | tf_op jit(solution)/shard_map/ppermute | solution.py:166
  71.0 0.0 collective-permute-done.1.upper
  71.0 2.5 %collective-permute-done.2.lower = s16[8,72,128]{2,1,0:T(8,128)(2,1)S(1)} collective-permute-done((s16[8,72,128]{2,1,0:T(8,128)(2,1)S(1)}, s16[8,72,128]{2,1,0:T(8,128)(2,1)S(1)}, u32[]{:S(2)}, u32[]{:S(2)}) %collective-permute-start.2) | collective-permute-done | bytes 147488 | tf_op jit(solution)/shard_map/ppermute | solution.py:166
  73.5 0.3 take.1
  73.8 31.2 %all_to_all.16.pieces = s16[8,136,128]{2,1,0:T(8,128)(2,1)S(1)} all-to-all(s16[8,136,128]{2,1,0:T(8,128)(2,1)S(1)} %take.1), channel_id=1, replica_groups=mesh['group'=16,'zh'=8,'zl'=2,'core'=2] {'zh'}, dimensions={0} | all-to-all | bytes 557056 | tf_op jit(solution)/shard_map/all_to_all | solution.py:168
  105.0 0.7 finish.1
  (6 shorter events, 0.1 us)
Async XLA Ops:
  1.4 13.9 %all-to-all-start = ((s32[16,1,4]{2,1,0:T(1,128)}), s32[16,1,4]{2,1,0:T(1,128)S(1)}, u32[]{:S(2)}, u32[]{:S(2)}) async-start(s32[16,1,4]{2,1,0:T(1,128)} %copy.7), calls=%async_computation | async-start | bytes 16384 | tf_op jit(solution)/shard_map/all_to_all | solution.py:178
  46.3 11.0 %collective-permute-start = (f32[16,128,128]{2,1,0:T(8,128)S(1)}, f32[16,128,128]{2,1,0:T(8,128)S(1)}, u32[]{:S(2)}, u32[]{:S(2)}) collective-permute-start(f32[16,128,128]{2,1,0:T(8,128)S(1)} %contract_0.1), channel_id=1, source_target_pairs={{0,1},{1,0},{2,3},{3,2},{4,5},{5,4},{6,7},{7,6},{8,9},{9,8},{10,11... | collective-permute-start | bytes 3145736 | tf_op jit(solution)/shard_map/ppermute | solution.py:188
  57.5 13.5 %collective-permute-start.1 = (s16[8,72,128]{2,1,0:T(8,128)(2,1)S(1)}, s16[8,72,128]{2,1,0:T(8,128)(2,1)S(1)}, u32[]{:S(2)}, u32[]{:S(2)}) collective-permute-start(s16[8,72,128]{2,1,0:T(8,128)(2,1)S(1)} %get-tuple-element.17), channel_id=1, source_target_pairs={{0,2},{2,0},{4,6},{6,4},{8,10},{10,8},{12,14},{14,12},{16,18},{18,... | collective-permute-start | bytes 442376 | tf_op jit(solution)/shard_map/ppermute | solution.py:165
  61.9 11.7 %collective-permute-start.2 = (s16[8,72,128]{2,1,0:T(8,128)(2,1)S(1)}, s16[8,72,128]{2,1,0:T(8,128)(2,1)S(1)}, u32[]{:S(2)}, u32[]{:S(2)}) collective-permute-start(s16[8,72,128]{2,1,0:T(8,128)(2,1)S(1)} %get-tuple-element.18), channel_id=1, source_target_pairs={{0,30},{2,4},{4,2},{6,8},{8,6},{10,12},{12,10},{14,16},{16,14},{18... | collective-permute-start | bytes 442376 | tf_op jit(solution)/shard_map/ppermute | solution.py:166

commit v4 on v3

--- a/solution.py
+++ b/solution.py
@@ -8,13 +8,13 @@
 from jax.sharding import Mesh
 from jax.sharding import PartitionSpec as P
 
-GROUP_MEMBER = ("group", "zh", "zl", "core")
-Z = ("zh", "zl")
+GROUP_MEMBER = ("group", "z", "core")
 PAIR = 2
 UNROLL = 8
 SLOTS = 512
 TOP = 32760.0
 SCALE_ROWS = 8
+SPLIT_LEVELS = 1
 STEPS = 128.0
 
 
@@ -44,12 +44,12 @@
     )(wanted, local)
 
 
-def task_tables(tasks, counts, core, parity, tiles, blank):
+def task_tables(tasks, counts, core, tiles, blank):
     a, s, r = tasks.T
     half = tiles // 2
     k = jnp.arange(tasks.shape[0], dtype=jnp.int32)
     valid = k < counts[0]
-    side = ((r & 1) ^ core ^ 1) * half + (((r >> 1) & 1) ^ parity ^ 1) * (half // 2) + (r >> 2)
+    side = ((r & 1) ^ core ^ 1) * half + (r >> 1)
     q = jnp.where(valid, side, tiles)
     code = a + s * 32
     rank = jnp.sum(((q[:, None] == q[None, :]) & (k[None, :] < k[:, None])).astype(jnp.int32), 1)
@@ -127,57 +127,66 @@
     return codes * (jnp.exp2(scale * (1.0 / STEPS)) * (1.0 / TOP))
 
 
-def plain_call(kernel, name, outs, *args):
+def fold_kernel(level, sources, inbox, z, *refs):
+    held, arrived, (kept, *sent) = refs[:sources], refs[sources : sources + inbox], refs[sources + inbox :]
+    bit = (z[0] >> level) & 1
+
+    def tile(i):
+        total = held[0][i]
+        for more in held[1:]:
+            total = total + more[i]
+        if arrived:
+            pieces = [load_coded(box, i) for box in arrived]
+            total = total + (jnp.concatenate(pieces, axis=0) if len(pieces) > 1 else pieces[0])
+        return total
+
+    if not sent:
+        kept[0] = tile(0)
+        return
+    for i in range(kept.shape[0]):
+        kept[i] = tile(2 * i + bit)
+        away = tile(2 * i + 1 - bit)
+        rows = away.shape[0] // len(sent)
+        for n, box in enumerate(sent):
+            store_coded(away[n * rows : (n + 1) * rows], box, i)
+
+
+def fold(level, z, held, arrived, tiles, size, parts):
+    f32 = jax.ShapeDtypeStruct((max(tiles // 2, 1), size, size), jnp.float32)
+    box = jax.ShapeDtypeStruct((tiles // 2, size // max(parts, 1) + SCALE_ROWS, size), jnp.int16)
+    vmem = pl.BlockSpec()
     return pl.pallas_call(
-        kernel,
-        out_shape=outs,
+        functools.partial(fold_kernel, level, len(held), len(arrived)),
+        out_shape=[f32] + [box] * parts,
+        in_specs=[pl.BlockSpec(memory_space=pltpu.SMEM)] + [vmem] * (len(held) + len(arrived)),
         compiler_params=pltpu.CompilerParams(vmem_limit_bytes=8 << 20),
         cost_estimate=pl.CostEstimate(flops=1 << 20, bytes_accessed=2 << 20, transcendentals=0),
-        name=name,
-    )(*args)
-
-
-def give_kernel(own, other, upper, lower):
-    mid = own.shape[1] // 2
-    for i in range(upper.shape[0]):
-        store_coded(own[i, :mid] + other[i, :mid], upper, i)
-        store_coded(own[i, mid:] + other[i, mid:], lower, i)
-
-
-def take_kernel(own, other, upper, lower, out):
-    for i in range(upper.shape[0]):
-        k = upper.shape[0] + i
-        more = jnp.concatenate([load_coded(upper, i), load_coded(lower, i)], axis=0)
-        store_coded(own[k] + other[k] + more, out, i)
-
-
-def finish_kernel(pieces, out):
-    total = load_coded(pieces, 0)
-    for i in range(1, pieces.shape[0]):
-        total += load_coded(pieces, i)
-    out[0] = total
+        name="fold_%d" % level,
+    )(z, *held, *arrived)
 
 
 def reduce_members(own, other):
     tiles, size, _ = own.shape
-    coded = lambda rows: jax.ShapeDtypeStruct((tiles // 2, rows + SCALE_ROWS, size), jnp.int16)
-    upper, lower = plain_call(give_kernel, "give", [coded(size // 2)] * 2, own, other)
-    upper = lax.ppermute(upper, Z, [(z, z ^ 1) for z in range(tiles)])
-    lower = lax.ppermute(lower, Z, [(z, (z + 1 if z % 2 else z - 1) % tiles) for z in range(tiles)])
-    pieces = plain_call(take_kernel, "take", coded(size), own, other, upper, lower)
-    pieces = lax.all_to_all(pieces, "zh", split_axis=0, concat_axis=0, tiled=True)
-    return plain_call(
-        finish_kernel, "finish", jax.ShapeDtypeStruct((1, size, size), jnp.float32), pieces
-    )
+    z = lax.axis_index("z").astype(jnp.int32).reshape(1)
+    held, arrived, level = [own, other], [], 0
+    count = tiles
+    while count > 1:
+        step = 1 << level
+        near = [(i, i ^ step) for i in range(tiles)]
+        far = [(i, (i + step if i & step else i - step) % tiles) for i in range(tiles)]
+        routes = [near, far] if level < SPLIT_LEVELS else [near]
+        kept, *boxes = fold(level, z, held, arrived, count, size, len(routes))
+        held, arrived = [kept], [lax.ppermute(b, "z", r) for b, r in zip(boxes, routes)]
+        level, count = level + 1, count // 2
+    return fold(level, z, held, arrived, count, size, 0)[0]
 
 
 def per_device(amplitudes, integrals, tasks, requests, counts):
     amount, tile, _ = amplitudes.shape
-    half = lax.axis_size(Z)
+    half = lax.axis_size("z")
     asked = requests.reshape(requests.shape[0], 1, requests.shape[1])
     wanted = lax.all_to_all(asked, "group", split_axis=0, concat_axis=0, tiled=True)
-    core, parity = lax.axis_index("core"), lax.axis_index("zl")
-    tables = task_tables(tasks, counts, core, parity, 2 * half, amount)
+    tables = task_tables(tasks, counts, lax.axis_index("core"), 2 * half, amount)
     blank = jnp.zeros((1, tile, tile), amplitudes.dtype)
     local = jnp.concatenate([amplitudes, blank, integrals])
     wanted, tables, local = lax.optimization_barrier((wanted, tables, local))
@@ -191,7 +200,7 @@
 
 
 def solution(mesh):
-    finer = Mesh(mesh.devices.reshape(mesh.shape["group"], 8, 2, 2), GROUP_MEMBER)
+    finer = Mesh(mesh.devices.reshape(mesh.shape["group"], 16, 2), GROUP_MEMBER)
     placed = (
         P(GROUP_MEMBER, None, None),
         P(GROUP_MEMBER, None, None),

time: 106 us -> 113 us (1.066); the launches traced: 106 us -> 111 us
  blocking collectives: 60 us -> 28.8 us
  waiting for transfers between devices: 5.74 us -> 30.9 us
  starting transfers between devices: 29.8 us -> 38.3 us
  Pallas kernels: 4.95 us -> 8.11 us
    all_to_all x1 -> x0, blocking collectives: 31.2 us -> none  [reduce_members(): lax.all_to_all(pieces, 'zh', split_axis=0, concat_axis=0, tiled=True)]
    ppermute x2 -> x5, waiting for transfers between devices: 2.51 us -> 27.6 us  [reduce_members(): lax.ppermute(b, 'z', r)]
    ppermute x2 -> x5, starting transfers between devices: 13.5 us -> 25 us  [reduce_members(): lax.ppermute(b, 'z', r)]
    ppermute x1, starting transfers between devices: 8.74 us -> 5.69 us  [per_device(): other = lax.ppermute(other, 'core', [(0, 1), (1, 0)])]
    pallas_call x2, Pallas kernels: 2.98 us -> 4.83 us  [contract(): pl.pallas_call(functools.partial(contract_kernel, which, half), grid_spec...]
    pallas_call x3 -> x5, Pallas kernels: 1.17 us -> 2.48 us  [fold(): pl.pallas_call(functools.partial(fold_kernel, level, len(held), len(arriv...]
  transfers between devices with their start and end apart: 4 -> 7, of which waited for: 3 -> 6; matrix products, arithmetic and copies ran while one was open for 3% -> 3% of each run, Pallas kernels for 2% -> 2%
where the time goes in v4:
time: 113 us; the launch traced here: 111 us
  starting transfers between devices  38.3 us (34%)
  waiting for transfers between devices  30.9 us (27%)
  blocking collectives  28.8 us (25%)
  Pallas kernels  8.11 us (7%)
  other arithmetic  2.95 us (3%)
  local copies, waits for them, and re-layouts  1.43 us (1%)
    all_to_all x1, blocking collectives, per_device(): lax.all_to_all(select(wanted, local, amount + 1), 'group', split_axis=0,...  28.8 us
    ppermute x5, waiting for transfers between devices, reduce_members(): lax.ppermute(b, 'z', r)  27.6 us
    ppermute x5, starting transfers between devices, reduce_members(): lax.ppermute(b, 'z', r)  25 us
    all_to_all x1, starting transfers between devices, per_device(): lax.all_to_all(asked, 'group', split_axis=0, concat_axis=0, tiled=True)  7.58 us
    ppermute x1, starting transfers between devices, per_device(): other = lax.ppermute(other, 'core', [(0, 1), (1, 0)])  5.69 us
    pallas_call x2, Pallas kernels, contract(): pl.pallas_call(functools.partial(contract_kernel, which, half), grid_spec...  4.83 us
    all_to_all x1, waiting for transfers between devices, per_device(): lax.all_to_all(asked, 'group', split_axis=0, concat_axis=0, tiled=True)  2.62 us
    pallas_call x5, Pallas kernels, fold(): pl.pallas_call(functools.partial(fold_kernel, level, len(held), len(arriv...  2.48 us
  transfers between devices with their start and end apart: 7, of which 6 were waited for; matrix products, arithmetic and copies ran while one was open for 3% of the time, Pallas kernels for 2%

profile of v4, /device:TPU:1, one launch (start us, length us, event | category | flops | bytes accessed | tf_op | source)
XLA Modules:
  0.0 111.3 jit_solution(326363649339191222)
XLA Ops:
  0.0 1.4 %copy.7 = s32[16,1,4]{2,1,0:T(1,128)} copy(s32[16,1,4]{0,2,1:T(4,128)} %bitcast.9) | data formatting | bytes 512 | tf_op jit(solution)/shard_map/reshape | solution.py:187
  1.4 7.6 %all-to-all-start = ((s32[16,1,4]{2,1,0:T(1,128)}), s32[16,1,4]{2,1,0:T(1,128)S(1)}, u32[]{:S(2)}, u32[]{:S(2)}) async-start(s32[16,1,4]{2,1,0:T(1,128)} %copy.7), calls=%async_computation | async-start | bytes 16384 | tf_op jit(solution)/shard_map/all_to_all | solution.py:188
  9.6 0.8 shift-right-arithmetic_add_fusion
  10.5 0.1 convert_reduce_fusion.1
  10.6 0.2 convert_reduce_fusion
  10.8 0.1 select_reduce_fusion.2.ends
  10.9 0.1 select_reduce_fusion.1
  11.0 0.2 select_reduce_fusion
  11.2 0.1 pad.1.clone
  11.3 1.3 %pad_maximum_fusion.local.amps = bf16[25,128,128]{2,1,0:T(8,128)(2,1)S(1)} fusion(bf16[8,128,128]{2,1,0:T(8,128)(2,1)} %param.6, bf16[16,128,128]{2,1,0:T(8,128)(2,1)} %param.5, bf16[25]{0:T(256)(128)(2,1)S(1)} %pad.1.clone), kind=kLoop, calls=%fused_computation | loop fusion | flops 819200 | bytes 1605682 | tf_op jit(solution)/shard_map/concatenate | solution.py:191
  12.6 0.1 convert_reduce_fusion.2.target
  12.7 2.6 %all-to-all-done.wanted = s32[16,1,4]{2,1,0:T(1,128)S(1)} async-done(((s32[16,1,4]{2,1,0:T(1,128)}), s32[16,1,4]{2,1,0:T(1,128)S(1)}, u32[]{:S(2)}, u32[]{:S(2)}) %all-to-all-start) | async-done | bytes 288 | tf_op jit(solution)/shard_map/all_to_all | solution.py:188
  15.3 0.8 select.31
  16.1 28.8 %all_to_all.10.fetched = bf16[64,128,128]{2,1,0:T(8,128)(2,1)S(1)} all-to-all(bf16[64,128,128]{2,1,0:T(8,128)(2,1)S(1)} %select.31), channel_id=1, replica_groups=mesh['group'=16,'z'=16,'core'=2] {'group'}, dimensions={0} | all-to-all | bytes 4194304 | tf_op jit(solution)/shard_map/all_to_all | solution.py:193
  44.9 2.9 %contract_0.1 = f32[16,128,128]{2,1,0:T(8,128)} custom-call(s32[512]{0:T(512)S(1)} %broadcast_add_fusion.table, s32[256]{0:T(256)S(1)} %convert_reduce_fusion.2.target, s32[32]{0:T(128)S(1)} %select_reduce_fusion.2.ends, bf16[25,128,128]{2,1,0:T(8,128)(2,1)S(1)} %pad_maximum_fusion.local.amps, bf16[64,128,128]{2,1,0:T(8,128)(2,1)S(1)} %all_to_all.10.fetched), custom_call_target="tpu_custom_call" | custom-call | flops 4294967296 | bytes 4194304 | tf_op jit(solution)/shard_map/contract_0/pallas_call | solution.py:95
  47.8 5.7 %collective-permute-start = (f32[16,128,128]{2,1,0:T(8,128)}, f32[16,128,128]{2,1,0:T(8,128)}, u32[]{:S(2)}, u32[]{:S(2)}) collective-permute-start(f32[16,128,128]{2,1,0:T(8,128)} %contract_0.1), channel_id=1, source_target_pairs={{0,1},{1,0},{2,3},{3,2},{4,5},{5,4},{6,7},{7,6},{8,9},{9,8},{10,11... | collective-permute-start | bytes 3145736 | tf_op jit(solution)/shard_map/ppermute | solution.py:197
  53.5 1.9 %contract_1.1.refs_0_ = f32[16,128,128]{2,1,0:T(8,128)S(1)} custom-call(s32[512]{0:T(512)S(1)} %broadcast_add_fusion.table, s32[256]{0:T(256)S(1)} %convert_reduce_fusion.2.target, s32[32]{0:T(128)S(1)} %select_reduce_fusion.2.ends, bf16[25,128,128]{2,1,0:T(8,128)(2,1)S(1)} %pad_maximum_fusion.local.amps, bf16[64,128,128]{2,1,0:T(8,128)(2,1)S(1)} %all_to_all.10.fetched), custom_call_target="tpu_custom_call" | custom-call | flops 4294967296 | bytes 4194304 | tf_op jit(solution)/shard_map/contract_1/pallas_call | solution.py:95
  55.5 0.7 collective-permute-done.refs_1_
  56.1 1.5 %fold_0.1 = (f32[8,128,128]{2,1,0:T(8,128)S(1)}, s16[8,72,128]{2,1,0:T(8,128)(2,1)S(1)}, s16[8,72,128]{2,1,0:T(8,128)(2,1)S(1)}) custom-call(s32[1]{0:T(128)} %bitcast.z, f32[16,128,128]{2,1,0:T(8,128)S(1)} %contract_1.1.refs_0_, f32[16,128,128]{2,1,0:T(8,128)} %collective-permute-done.refs_1_), custom_call_target="tpu_custom_call" | custom-call | flops 1048576 | bytes 2097152 | tf_op jit(solution)/shard_map/fold_0/pallas_call | solution.py:158
  57.6 3.6 %collective-permute-start.1 = (s16[8,72,128]{2,1,0:T(8,128)(2,1)S(1)}, s16[8,72,128]{2,1,0:T(8,128)(2,1)S(1)}, u32[]{:S(2)}, u32[]{:S(2)}) collective-permute-start(s16[8,72,128]{2,1,0:T(8,128)(2,1)S(1)} %get-tuple-element.25), channel_id=1, source_target_pairs={{0,2},{2,0},{4,6},{6,4},{8,10},{10,8},{12,14},{14,12},{16,18},{18,... | collective-permute-start | bytes 442376 | tf_op jit(solution)/shard_map/ppermute | solution.py:179
  61.2 12.0 %collective-permute-start.2 = (s16[8,72,128]{2,1,0:T(8,128)(2,1)S(1)}, s16[8,72,128]{2,1,0:T(8,128)(2,1)S(1)}, u32[]{:S(2)}, u32[]{:S(2)}) collective-permute-start(s16[8,72,128]{2,1,0:T(8,128)(2,1)S(1)} %get-tuple-element.26), channel_id=1, source_target_pairs={{0,30},{2,4},{4,2},{6,8},{8,6},{10,12},{12,10},{14,16},{16,14},{18... | collective-permute-start | bytes 442376 | tf_op jit(solution)/shard_map/ppermute | solution.py:179
  73.2 0.0 collective-permute-done.1.refs_1_
  73.2 3.8 %collective-permute-done.2.refs_2_ = s16[8,72,128]{2,1,0:T(8,128)(2,1)S(1)} collective-permute-done((s16[8,72,128]{2,1,0:T(8,128)(2,1)S(1)}, s16[8,72,128]{2,1,0:T(8,128)(2,1)S(1)}, u32[]{:S(2)}, u32[]{:S(2)}) %collective-permute-start.2) | collective-permute-done | bytes 147488 | tf_op jit(solution)/shard_map/ppermute | solution.py:179
  77.0 0.2 fold_1.1
  77.2 1.9 %collective-permute-start.3 = (s16[4,136,128]{2,1,0:T(8,128)(2,1)S(1)}, s16[4,136,128]{2,1,0:T(8,128)(2,1)S(1)}, u32[]{:S(2)}, u32[]{:S(2)}) collective-permute-start(s16[4,136,128]{2,1,0:T(8,128)(2,1)S(1)} %get-tuple-element.28), channel_id=1, source_target_pairs={{0,4},{2,6},{4,0},{6,2},{8,12},{10,14},{12,8},{14,10},{16,20},{18,... | collective-permute-start | bytes 417800 | tf_op jit(solution)/shard_map/ppermute | solution.py:179
  79.1 4.8 %collective-permute-done.3.refs_1_ = s16[4,136,128]{2,1,0:T(8,128)(2,1)S(1)} collective-permute-done((s16[4,136,128]{2,1,0:T(8,128)(2,1)S(1)}, s16[4,136,128]{2,1,0:T(8,128)(2,1)S(1)}, u32[]{:S(2)}, u32[]{:S(2)}) %collective-permute-start.3) | collective-permute-done | bytes 139296 | tf_op jit(solution)/shard_map/ppermute | solution.py:179
  83.9 0.1 fold_2.1
  84.0 5.1 %collective-permute-start.4 = (s16[2,136,128]{2,1,0:T(8,128)(2,1)S(1)}, s16[2,136,128]{2,1,0:T(8,128)(2,1)S(1)}, u32[]{:S(2)}, u32[]{:S(2)}) collective-permute-start(s16[2,136,128]{2,1,0:T(8,128)(2,1)S(1)} %get-tuple-element.30), channel_id=1, source_target_pairs={{0,8},{2,10},{4,12},{6,14},{8,0},{10,2},{12,4},{14,6},{16,24},{18,... | collective-permute-start | bytes 208904 | tf_op jit(solution)/shard_map/ppermute | solution.py:179
  89.1 8.0 %collective-permute-done.4.refs_1_ = s16[2,136,128]{2,1,0:T(8,128)(2,1)S(1)} collective-permute-done((s16[2,136,128]{2,1,0:T(8,128)(2,1)S(1)}, s16[2,136,128]{2,1,0:T(8,128)(2,1)S(1)}, u32[]{:S(2)}, u32[]{:S(2)}) %collective-permute-start.4) | collective-permute-done | bytes 69664 | tf_op jit(solution)/shard_map/ppermute | solution.py:179
  97.2 0.1 fold_3.1
  97.2 2.4 %collective-permute-start.5 = (s16[1,136,128]{2,1,0:T(8,128)(2,1)S(1)}, s16[1,136,128]{2,1,0:T(8,128)(2,1)S(1)}, u32[]{:S(2)}, u32[]{:S(2)}) collective-permute-start(s16[1,136,128]{2,1,0:T(8,128)(2,1)S(1)} %get-tuple-element.32), channel_id=1, source_target_pairs={{0,16},{2,18},{4,20},{6,22},{8,24},{10,26},{12,28},{14,30},{16,0},... | collective-permute-start | bytes 104456 | tf_op jit(solution)/shard_map/ppermute | solution.py:179
  99.7 11.0 %collective-permute-done.5.refs_1_ = s16[1,136,128]{2,1,0:T(8,128)(2,1)S(1)} collective-permute-done((s16[1,136,128]{2,1,0:T(8,128)(2,1)S(1)}, s16[1,136,128]{2,1,0:T(8,128)(2,1)S(1)}, u32[]{:S(2)}, u32[]{:S(2)}) %collective-permute-start.5) | collective-permute-done | bytes 34848 | tf_op jit(solution)/shard_map/ppermute | solution.py:179
  110.6 0.6 fold_4.1
  (6 shorter events, 0.1 us)
Async XLA Ops:
  1.4 13.9 %all-to-all-start = ((s32[16,1,4]{2,1,0:T(1,128)}), s32[16,1,4]{2,1,0:T(1,128)S(1)}, u32[]{:S(2)}, u32[]{:S(2)}) async-start(s32[16,1,4]{2,1,0:T(1,128)} %copy.7), calls=%async_computation | async-start | bytes 16384 | tf_op jit(solution)/shard_map/all_to_all | solution.py:188
  47.8 8.3 %collective-permute-start = (f32[16,128,128]{2,1,0:T(8,128)}, f32[16,128,128]{2,1,0:T(8,128)}, u32[]{:S(2)}, u32[]{:S(2)}) collective-permute-start(f32[16,128,128]{2,1,0:T(8,128)} %contract_0.1), channel_id=1, source_target_pairs={{0,1},{1,0},{2,3},{3,2},{4,5},{5,4},{6,7},{7,6},{8,9},{9,8},{10,11... | collective-permute-start | bytes 3145736 | tf_op jit(solution)/shard_map/ppermute | solution.py:197
  57.6 15.6 %collective-permute-start.1 = (s16[8,72,128]{2,1,0:T(8,128)(2,1)S(1)}, s16[8,72,128]{2,1,0:T(8,128)(2,1)S(1)}, u32[]{:S(2)}, u32[]{:S(2)}) collective-permute-start(s16[8,72,128]{2,1,0:T(8,128)(2,1)S(1)} %get-tuple-element.25), channel_id=1, source_target_pairs={{0,2},{2,0},{4,6},{6,4},{8,10},{10,8},{12,14},{14,12},{16,18},{18,... | collective-permute-start | bytes 442376 | tf_op jit(solution)/shard_map/ppermute | solution.py:179
  61.2 15.8 %collective-permute-start.2 = (s16[8,72,128]{2,1,0:T(8,128)(2,1)S(1)}, s16[8,72,128]{2,1,0:T(8,128)(2,1)S(1)}, u32[]{:S(2)}, u32[]{:S(2)}) collective-permute-start(s16[8,72,128]{2,1,0:T(8,128)(2,1)S(1)} %get-tuple-element.26), channel_id=1, source_target_pairs={{0,30},{2,4},{4,2},{6,8},{8,6},{10,12},{12,10},{14,16},{16,14},{18... | collective-permute-start | bytes 442376 | tf_op jit(solution)/shard_map/ppermute | solution.py:179
  77.2 6.7 %collective-permute-start.3 = (s16[4,136,128]{2,1,0:T(8,128)(2,1)S(1)}, s16[4,136,128]{2,1,0:T(8,128)(2,1)S(1)}, u32[]{:S(2)}, u32[]{:S(2)}) collective-permute-start(s16[4,136,128]{2,1,0:T(8,128)(2,1)S(1)} %get-tuple-element.28), channel_id=1, source_target_pairs={{0,4},{2,6},{4,0},{6,2},{8,12},{10,14},{12,8},{14,10},{16,20},{18,... | collective-permute-start | bytes 417800 | tf_op jit(solution)/shard_map/ppermute | solution.py:179
  84.0 13.2 %collective-permute-start.4 = (s16[2,136,128]{2,1,0:T(8,128)(2,1)S(1)}, s16[2,136,128]{2,1,0:T(8,128)(2,1)S(1)}, u32[]{:S(2)}, u32[]{:S(2)}) collective-permute-start(s16[2,136,128]{2,1,0:T(8,128)(2,1)S(1)} %get-tuple-element.30), channel_id=1, source_target_pairs={{0,8},{2,10},{4,12},{6,14},{8,0},{10,2},{12,4},{14,6},{16,24},{18,... | collective-permute-start | bytes 208904 | tf_op jit(solution)/shard_map/ppermute | solution.py:179
  97.2 13.4 %collective-permute-start.5 = (s16[1,136,128]{2,1,0:T(8,128)(2,1)S(1)}, s16[1,136,128]{2,1,0:T(8,128)(2,1)S(1)}, u32[]{:S(2)}, u32[]{:S(2)}) collective-permute-start(s16[1,136,128]{2,1,0:T(8,128)(2,1)S(1)} %get-tuple-element.32), channel_id=1, source_target_pairs={{0,16},{2,18},{4,20},{6,22},{8,24},{10,26},{12,28},{14,30},{16,0},... | collective-permute-start | bytes 104456 | tf_op jit(solution)/shard_map/ppermute | solution.py:179

commit v5 on v3

--- a/solution.py
+++ b/solution.py
@@ -11,7 +11,7 @@
 GROUP_MEMBER = ("group", "zh", "zl", "core")
 Z = ("zh", "zl")
 PAIR = 2
-UNROLL = 8
+UNROLL = 24
 SLOTS = 512
 TOP = 32760.0
 SCALE_ROWS = 8
@@ -66,40 +66,37 @@
     return table, target, ends
 
 
-def contract_kernel(which, half, table, target, ends, amps, fetched, out, acc):
+def contract_kernel(which, half, blank, table, target, ends, amps, fetched, out):
     low = ends[half - 1] if which else 0
     high = ends[which * half + half - 1]
-    acc[...] = jnp.zeros_like(acc)
+    out[...] = jnp.zeros_like(out)
 
     def step(i, carry):
         products = []
         for u in range(UNROLL):
             j = low + i * UNROLL + u
-            codes = [table[j * PAIR + n] for n in range(PAIR)]
+            codes = [jnp.where(j < high, table[j * PAIR + n], blank) for n in range(PAIR)]
             left = jnp.concatenate([amps[c & 31] for c in codes], axis=1)
             right = jnp.concatenate([fetched[c >> 5] for c in codes], axis=0)
             products.append(jnp.dot(left, right, preferred_element_type=jnp.float32))
         for u in range(UNROLL):
             j = low + i * UNROLL + u
-            tile = jnp.where(j < high, target[j] - which * half, half)
-            acc[tile] += products[u]
+            out[jnp.minimum(target[j] - which * half, half - 1)] += products[u]
         return carry
 
     lax.fori_loop(0, (high - low + UNROLL - 1) // UNROLL, step, 0)
-    out[...] = acc[:half]
-
-
-def contract(which, tables, amps, fetched, half):
+
+
+def contract(which, tables, amps, fetched, half, blank):
     size = amps.shape[1]
     full = lambda n: pl.BlockSpec((n, size, size), lambda i, *_: (0, 0, 0))
     return pl.pallas_call(
-        functools.partial(contract_kernel, which, half),
+        functools.partial(contract_kernel, which, half, blank),
         grid_spec=pltpu.PrefetchScalarGridSpec(
             num_scalar_prefetch=3,
             grid=(1,),
             in_specs=[full(amps.shape[0]), full(fetched.shape[0])],
             out_specs=full(half),
-            scratch_shapes=[pltpu.VMEM((half + 1, size, size), jnp.float32)],
         ),
         out_shape=jax.ShapeDtypeStruct((half, size, size), jnp.float32),
         compiler_params=pltpu.CompilerParams(vmem_limit_bytes=16 << 20),
@@ -137,18 +134,15 @@
     )(*args)
 
 
-def give_kernel(own, other, upper, lower):
-    mid = own.shape[1] // 2
-    for i in range(upper.shape[0]):
-        store_coded(own[i, :mid] + other[i, :mid], upper, i)
-        store_coded(own[i, mid:] + other[i, mid:], lower, i)
-
-
-def take_kernel(own, other, upper, lower, out):
-    for i in range(upper.shape[0]):
-        k = upper.shape[0] + i
-        more = jnp.concatenate([load_coded(upper, i), load_coded(lower, i)], axis=0)
-        store_coded(own[k] + other[k] + more, out, i)
+def give_kernel(own, other, out):
+    for i in range(out.shape[0]):
+        store_coded(own[i] + other[i], out, i)
+
+
+def take_kernel(own, other, arrived, out):
+    for i in range(out.shape[0]):
+        k = out.shape[0] + i
+        store_coded(own[k] + other[k] + load_coded(arrived, i), out, i)
 
 
 def finish_kernel(pieces, out):
@@ -160,11 +154,10 @@
 
 def reduce_members(own, other):
     tiles, size, _ = own.shape
-    coded = lambda rows: jax.ShapeDtypeStruct((tiles // 2, rows + SCALE_ROWS, size), jnp.int16)
-    upper, lower = plain_call(give_kernel, "give", [coded(size // 2)] * 2, own, other)
-    upper = lax.ppermute(upper, Z, [(z, z ^ 1) for z in range(tiles)])
-    lower = lax.ppermute(lower, Z, [(z, (z + 1 if z % 2 else z - 1) % tiles) for z in range(tiles)])
-    pieces = plain_call(take_kernel, "take", coded(size), own, other, upper, lower)
+    coded = jax.ShapeDtypeStruct((tiles // 2, size + SCALE_ROWS, size), jnp.int16)
+    arrived = plain_call(give_kernel, "give", coded, own, other)
+    arrived = lax.ppermute(arrived, "zl", [(0, 1), (1, 0)])
+    pieces = plain_call(take_kernel, "take", coded, own, other, arrived)
     pieces = lax.all_to_all(pieces, "zh", split_axis=0, concat_axis=0, tiled=True)
     return plain_call(
         finish_kernel, "finish", jax.ShapeDtypeStruct((1, size, size), jnp.float32), pieces
@@ -184,9 +177,9 @@
     fetched = lax.all_to_all(
         select(wanted, local, amount + 1), "group", split_axis=0, concat_axis=0, tiled=True
     )
-    other = contract(0, tables, local, fetched, half)
+    other = contract(0, tables, local, fetched, half, amount)
     other = lax.ppermute(other, "core", [(0, 1), (1, 0)])
-    own = contract(1, tables, local, fetched, half)
+    own = contract(1, tables, local, fetched, half, amount)
     return reduce_members(own, other)
 
 

time: 106 us -> 103 us (0.972)
  the two profiles are of different devices: /device:TPU:1 before, /device:TPU:16 now
where the time goes in v5:
time: 103 us
  blocking collectives  67.4 us (65%)
  starting transfers between devices  14.2 us (14%)
  waiting for transfers between devices  8.97 us (9%)
  Pallas kernels  7.02 us (7%)
  other arithmetic  2.95 us (3%)
  local copies, waits for them, and re-layouts  1.43 us (1%)
    all_to_all x1, blocking collectives, reduce_members(): lax.all_to_all(pieces, 'zh', split_axis=0, concat_axis=0, tiled=True)  38.4 us
    all_to_all x1, blocking collectives, per_device(): lax.all_to_all(select(wanted, local, amount + 1), 'group', split_axis=0,...  29 us
    all_to_all x1, starting transfers between devices, per_device(): lax.all_to_all(asked, 'group', split_axis=0, concat_axis=0, tiled=True)  9.02 us
    ppermute x1, waiting for transfers between devices, reduce_members(): arrived = lax.ppermute(arrived, 'zl', [(0, 1), (1, 0)])  7.34 us
    pallas_call x2, Pallas kernels, contract(): pl.pallas_call(functools.partial(contract_kernel, which, half, blank), gr...  5.06 us
    ppermute x1, starting transfers between devices, reduce_members(): arrived = lax.ppermute(arrived, 'zl', [(0, 1), (1, 0)])  3.24 us
  transfers between devices with their start and end apart: 3, of which 3 were waited for; matrix products, arithmetic and copies ran while one was open for 3% of the time, Pallas kernels for 2%

profile of v5, /device:TPU:16, one launch (start us, length us, event | category | flops | bytes accessed | tf_op | source)
XLA Modules:
  0.0 102.7 jit_solution(9286191868098566527)
XLA Ops:
  0.0 1.4 %copy.7 = s32[16,1,4]{2,1,0:T(1,128)} copy(s32[16,1,4]{0,2,1:T(4,128)} %bitcast.8) | data formatting | bytes 512 | tf_op jit(solution)/shard_map/reshape | solution.py:170
  1.4 9.0 %all-to-all-start = ((s32[16,1,4]{2,1,0:T(1,128)}), s32[16,1,4]{2,1,0:T(1,128)S(1)}, u32[]{:S(2)}, u32[]{:S(2)}) async-start(s32[16,1,4]{2,1,0:T(1,128)} %copy.7), calls=%async_computation | async-start | bytes 16384 | tf_op jit(solution)/shard_map/all_to_all | solution.py:171
  11.0 0.8 add_add_fusion
  11.9 0.1 convert_reduce_fusion.1
  12.0 0.2 convert_reduce_fusion
  12.2 0.1 select_reduce_fusion.2.ends
  12.4 0.1 select_reduce_fusion.1
  12.5 0.2 select_reduce_fusion
  12.7 0.1 pad.1.clone
  12.7 1.3 %pad_maximum_fusion.local.amps = bf16[25,128,128]{2,1,0:T(8,128)(2,1)S(1)} fusion(bf16[8,128,128]{2,1,0:T(8,128)(2,1)} %param.6, bf16[16,128,128]{2,1,0:T(8,128)(2,1)} %param.5, bf16[25]{0:T(256)(128)(2,1)S(1)} %pad.1.clone), kind=kLoop, calls=%fused_computation | loop fusion | flops 819200 | bytes 1605682 | tf_op jit(solution)/shard_map/concatenate | solution.py:175
  14.0 0.1 convert_reduce_fusion.2.target
  14.1 1.5 %all-to-all-done.wanted = s32[16,1,4]{2,1,0:T(1,128)S(1)} async-done(((s32[16,1,4]{2,1,0:T(1,128)}), s32[16,1,4]{2,1,0:T(1,128)S(1)}, u32[]{:S(2)}, u32[]{:S(2)}) %all-to-all-start) | async-done | bytes 288 | tf_op jit(solution)/shard_map/all_to_all | solution.py:171
  15.6 0.8 select.31
  16.4 29.0 %all_to_all.15.fetched = bf16[64,128,128]{2,1,0:T(8,128)(2,1)S(1)} all-to-all(bf16[64,128,128]{2,1,0:T(8,128)(2,1)S(1)} %select.31), channel_id=1, replica_groups=mesh['group'=16,'zh'=8,'zl'=2,'core'=2] {'group'}, dimensions={0} | all-to-all | bytes 4194304 | tf_op jit(solution)/shard_map/all_to_all | solution.py:177
  45.5 2.5 %contract_0.1 = f32[16,128,128]{2,1,0:T(8,128)S(1)} custom-call(s32[512]{0:T(512)S(1)} %broadcast_add_fusion.table, s32[256]{0:T(256)S(1)} %convert_reduce_fusion.2.target, s32[32]{0:T(128)S(1)} %select_reduce_fusion.2.ends, bf16[25,128,128]{2,1,0:T(8,128)(2,1)S(1)} %pad_maximum_fusion.local.amps, bf16[64,128,128]{2,1,0:T(8,128)(2,1)S(1)} %all_to_all.15.fetched), custom_call_target="tpu_custom_call" | custom-call | flops 4294967296 | bytes 4194304 | tf_op jit(solution)/shard_map/contract_0/pallas_call | solution.py:93
  48.0 1.9 %collective-permute-start = (f32[16,128,128]{2,1,0:T(8,128)S(1)}, f32[16,128,128]{2,1,0:T(8,128)S(1)}, u32[]{:S(2)}, u32[]{:S(2)}) collective-permute-start(f32[16,128,128]{2,1,0:T(8,128)S(1)} %contract_0.1), channel_id=1, source_target_pairs={{0,1},{1,0},{2,3},{3,2},{4,5},{5,4},{6,7},{7,6},{8,9},{9,8},{10,11... | collective-permute-start | bytes 3145736 | tf_op jit(solution)/shard_map/ppermute | solution.py:181
  49.9 2.5 %contract_1.1.own = f32[16,128,128]{2,1,0:T(8,128)S(1)} custom-call(s32[512]{0:T(512)S(1)} %broadcast_add_fusion.table, s32[256]{0:T(256)S(1)} %convert_reduce_fusion.2.target, s32[32]{0:T(128)S(1)} %select_reduce_fusion.2.ends, bf16[25,128,128]{2,1,0:T(8,128)(2,1)S(1)} %pad_maximum_fusion.local.amps, bf16[64,128,128]{2,1,0:T(8,128)(2,1)S(1)} %all_to_all.15.fetched), custom_call_target="tpu_custom_call" | custom-call | flops 4294967296 | bytes 4194304 | tf_op jit(solution)/shard_map/contract_1/pallas_call | solution.py:93
  52.5 0.1 collective-permute-done.other
  52.6 0.2 give.1
  52.8 3.2 %collective-permute-start.1 = (s16[8,136,128]{2,1,0:T(8,128)(2,1)S(1)}, s16[8,136,128]{2,1,0:T(8,128)(2,1)S(1)}, u32[]{:S(2)}, u32[]{:S(2)}) collective-permute-start(s16[8,136,128]{2,1,0:T(8,128)(2,1)S(1)} %give.1), channel_id=1, source_target_pairs={{0,2},{2,0},{1,3},{3,1},{4,6},{6,4},{5,7},{7,5},{8,10},{10,8},{9,1... | collective-permute-start | bytes 835592 | tf_op jit(solution)/shard_map/ppermute | solution.py:159
  56.0 7.3 %collective-permute-done.1.arrived = s16[8,136,128]{2,1,0:T(8,128)(2,1)S(1)} collective-permute-done((s16[8,136,128]{2,1,0:T(8,128)(2,1)S(1)}, s16[8,136,128]{2,1,0:T(8,128)(2,1)S(1)}, u32[]{:S(2)}, u32[]{:S(2)}) %collective-permute-start.1) | collective-permute-done | bytes 278560 | tf_op jit(solution)/shard_map/ppermute | solution.py:159
  63.4 0.3 take.1
  63.6 38.4 %all_to_all.16.pieces = s16[8,136,128]{2,1,0:T(8,128)(2,1)S(1)} all-to-all(s16[8,136,128]{2,1,0:T(8,128)(2,1)S(1)} %take.1), channel_id=1, replica_groups=mesh['group'=16,'zh'=8,'zl'=2,'core'=2] {'zh'}, dimensions={0} | all-to-all | bytes 557056 | tf_op jit(solution)/shard_map/all_to_all | solution.py:161
  102.0 0.7 finish.1
  (6 shorter events, 0.1 us)
Async XLA Ops:
  1.4 14.3 %all-to-all-start = ((s32[16,1,4]{2,1,0:T(1,128)}), s32[16,1,4]{2,1,0:T(1,128)S(1)}, u32[]{:S(2)}, u32[]{:S(2)}) async-start(s32[16,1,4]{2,1,0:T(1,128)} %copy.7), calls=%async_computation | async-start | bytes 16384 | tf_op jit(solution)/shard_map/all_to_all | solution.py:171
  48.0 4.6 %collective-permute-start = (f32[16,128,128]{2,1,0:T(8,128)S(1)}, f32[16,128,128]{2,1,0:T(8,128)S(1)}, u32[]{:S(2)}, u32[]{:S(2)}) collective-permute-start(f32[16,128,128]{2,1,0:T(8,128)S(1)} %contract_0.1), channel_id=1, source_target_pairs={{0,1},{1,0},{2,3},{3,2},{4,5},{5,4},{6,7},{7,6},{8,9},{9,8},{10,11... | collective-permute-start | bytes 3145736 | tf_op jit(solution)/shard_map/ppermute | solution.py:181
  52.8 10.6 %collective-permute-start.1 = (s16[8,136,128]{2,1,0:T(8,128)(2,1)S(1)}, s16[8,136,128]{2,1,0:T(8,128)(2,1)S(1)}, u32[]{:S(2)}, u32[]{:S(2)}) collective-permute-start(s16[8,136,128]{2,1,0:T(8,128)(2,1)S(1)} %give.1), channel_id=1, source_target_pairs={{0,2},{2,0},{1,3},{3,1},{4,6},{6,4},{5,7},{7,5},{8,10},{10,8},{9,1... | collective-permute-start | bytes 835592 | tf_op jit(solution)/shard_map/ppermute | solution.py:159

commit v6 on v5

--- a/solution.py
+++ b/solution.py
@@ -156,7 +156,11 @@
     tiles, size, _ = own.shape
     coded = jax.ShapeDtypeStruct((tiles // 2, size + SCALE_ROWS, size), jnp.int16)
     arrived = plain_call(give_kernel, "give", coded, own, other)
-    arrived = lax.ppermute(arrived, "zl", [(0, 1), (1, 0)])
+    route = []
+    for z in range(tiles):
+        route.append((2 * z, 2 * (z ^ 1)))
+        route.append((2 * z + 1, 2 * ((z + 1 if z % 2 else z - 1) % tiles) + 1))
+    arrived = lax.ppermute(arrived, (*Z, "core"), route)
     pieces = plain_call(take_kernel, "take", coded, own, other, arrived)
     pieces = lax.all_to_all(pieces, "zh", split_axis=0, concat_axis=0, tiled=True)
     return plain_call(

time: 103 us -> 101 us (0.981)
  the two profiles are of different devices: /device:TPU:16 before, /device:TPU:2 now
where the time goes in v6:
time: 101 us
  blocking collectives  67.7 us (67%)
  starting transfers between devices  14.9 us (15%)
  waiting for transfers between devices  8.46 us (8%)
  Pallas kernels  4.52 us (4%)
  other arithmetic  2.95 us (3%)
  local copies, waits for them, and re-layouts  1.43 us (1%)
    all_to_all x1, blocking collectives, reduce_members(): lax.all_to_all(pieces, 'zh', split_axis=0, concat_axis=0, tiled=True)  38.2 us
    all_to_all x1, blocking collectives, per_device(): lax.all_to_all(select(wanted, local, amount + 1), 'group', split_axis=0,...  29.5 us
    all_to_all x1, starting transfers between devices, per_device(): lax.all_to_all(asked, 'group', split_axis=0, concat_axis=0, tiled=True)  9.17 us
    ppermute x1, waiting for transfers between devices, reduce_members(): arrived = lax.ppermute(arrived, (*Z, 'core'), route)  4.65 us
    ppermute x1, starting transfers between devices, reduce_members(): arrived = lax.ppermute(arrived, (*Z, 'core'), route)  3.78 us
    pallas_call x2, Pallas kernels, contract(): pl.pallas_call(functools.partial(contract_kernel, which, half, blank), gr...  2.56 us
    all_to_all x1, waiting for transfers between devices, per_device(): lax.all_to_all(asked, 'group', split_axis=0, concat_axis=0, tiled=True)  2.47 us
  transfers between devices with their start and end apart: 3, of which 3 were waited for; matrix products, arithmetic and copies ran while one was open for 3% of the time, Pallas kernels for 1%

profile of v6, /device:TPU:2, one launch (start us, length us, event | category | flops | bytes accessed | tf_op | source)
XLA Modules:
  0.0 100.6 jit_solution(17378840312929659219)
XLA Ops:
  0.0 1.4 %copy.7 = s32[16,1,4]{2,1,0:T(1,128)} copy(s32[16,1,4]{0,2,1:T(4,128)} %bitcast.8) | data formatting | bytes 512 | tf_op jit(solution)/shard_map/reshape | solution.py:174
  1.4 9.2 %all-to-all-start = ((s32[16,1,4]{2,1,0:T(1,128)}), s32[16,1,4]{2,1,0:T(1,128)S(1)}, u32[]{:S(2)}, u32[]{:S(2)}) async-start(s32[16,1,4]{2,1,0:T(1,128)} %copy.7), calls=%async_computation | async-start | bytes 16384 | tf_op jit(solution)/shard_map/all_to_all | solution.py:175
  11.2 0.8 add_add_fusion
  12.0 0.1 convert_reduce_fusion.1
  12.2 0.2 convert_reduce_fusion
  12.4 0.1 select_reduce_fusion.2.ends
  12.5 0.1 select_reduce_fusion.1
  12.6 0.2 select_reduce_fusion
  12.8 0.1 pad.1.clone
  12.9 1.3 %pad_maximum_fusion.local.amps = bf16[25,128,128]{2,1,0:T(8,128)(2,1)S(1)} fusion(bf16[8,128,128]{2,1,0:T(8,128)(2,1)} %param.6, bf16[16,128,128]{2,1,0:T(8,128)(2,1)} %param.5, bf16[25]{0:T(256)(128)(2,1)S(1)} %pad.1.clone), kind=kLoop, calls=%fused_computation | loop fusion | flops 819200 | bytes 1605682 | tf_op jit(solution)/shard_map/concatenate | solution.py:179
  14.1 0.1 convert_reduce_fusion.2.target
  14.2 2.5 %all-to-all-done.wanted = s32[16,1,4]{2,1,0:T(1,128)S(1)} async-done(((s32[16,1,4]{2,1,0:T(1,128)}), s32[16,1,4]{2,1,0:T(1,128)S(1)}, u32[]{:S(2)}, u32[]{:S(2)}) %all-to-all-start) | async-done | bytes 288 | tf_op jit(solution)/shard_map/all_to_all | solution.py:175
  16.7 0.8 select.31
  17.5 29.5 %all_to_all.15.fetched = bf16[64,128,128]{2,1,0:T(8,128)(2,1)S(1)} all-to-all(bf16[64,128,128]{2,1,0:T(8,128)(2,1)S(1)} %select.31), channel_id=1, replica_groups=mesh['group'=16,'zh'=8,'zl'=2,'core'=2] {'group'}, dimensions={0} | all-to-all | bytes 4194304 | tf_op jit(solution)/shard_map/all_to_all | solution.py:181
  47.0 1.3 %contract_0.1 = f32[16,128,128]{2,1,0:T(8,128)S(1)} custom-call(s32[512]{0:T(512)S(1)} %broadcast_add_fusion.table, s32[256]{0:T(256)S(1)} %convert_reduce_fusion.2.target, s32[32]{0:T(128)S(1)} %select_reduce_fusion.2.ends, bf16[25,128,128]{2,1,0:T(8,128)(2,1)S(1)} %pad_maximum_fusion.local.amps, bf16[64,128,128]{2,1,0:T(8,128)(2,1)S(1)} %all_to_all.15.fetched), custom_call_target="tpu_custom_call" | custom-call | flops 4294967296 | bytes 4194304 | tf_op jit(solution)/shard_map/contract_0/pallas_call | solution.py:93
  48.3 1.9 %collective-permute-start = (f32[16,128,128]{2,1,0:T(8,128)S(1)}, f32[16,128,128]{2,1,0:T(8,128)S(1)}, u32[]{:S(2)}, u32[]{:S(2)}) collective-permute-start(f32[16,128,128]{2,1,0:T(8,128)S(1)} %contract_0.1), channel_id=1, source_target_pairs={{0,1},{1,0},{2,3},{3,2},{4,5},{5,4},{6,7},{7,6},{8,9},{9,8},{10,11... | collective-permute-start | bytes 3145736 | tf_op jit(solution)/shard_map/ppermute | solution.py:185
  50.2 1.3 %contract_1.1.own = f32[16,128,128]{2,1,0:T(8,128)S(1)} custom-call(s32[512]{0:T(512)S(1)} %broadcast_add_fusion.table, s32[256]{0:T(256)S(1)} %convert_reduce_fusion.2.target, s32[32]{0:T(128)S(1)} %select_reduce_fusion.2.ends, bf16[25,128,128]{2,1,0:T(8,128)(2,1)S(1)} %pad_maximum_fusion.local.amps, bf16[64,128,128]{2,1,0:T(8,128)(2,1)S(1)} %all_to_all.15.fetched), custom_call_target="tpu_custom_call" | custom-call | flops 4294967296 | bytes 4194304 | tf_op jit(solution)/shard_map/contract_1/pallas_call | solution.py:93
  51.5 1.3 %collective-permute-done.other = f32[16,128,128]{2,1,0:T(8,128)S(1)} collective-permute-done((f32[16,128,128]{2,1,0:T(8,128)S(1)}, f32[16,128,128]{2,1,0:T(8,128)S(1)}, u32[]{:S(2)}, u32[]{:S(2)}) %collective-permute-start) | collective-permute-done | bytes 1048608 | tf_op jit(solution)/shard_map/ppermute | solution.py:185
  52.9 0.2 give.1
  53.1 3.8 %collective-permute-start.1 = (s16[8,136,128]{2,1,0:T(8,128)(2,1)S(1)}, s16[8,136,128]{2,1,0:T(8,128)(2,1)S(1)}, u32[]{:S(2)}, u32[]{:S(2)}) collective-permute-start(s16[8,136,128]{2,1,0:T(8,128)(2,1)S(1)} %give.1), channel_id=1, source_target_pairs={{0,2},{1,31},{2,0},{3,5},{4,6},{5,3},{6,4},{7,9},{8,10},{9,7},{10,... | collective-permute-start | bytes 835592 | tf_op jit(solution)/shard_map/ppermute | solution.py:163
  56.8 4.7 %collective-permute-done.1.arrived = s16[8,136,128]{2,1,0:T(8,128)(2,1)S(1)} collective-permute-done((s16[8,136,128]{2,1,0:T(8,128)(2,1)S(1)}, s16[8,136,128]{2,1,0:T(8,128)(2,1)S(1)}, u32[]{:S(2)}, u32[]{:S(2)}) %collective-permute-start.1) | collective-permute-done | bytes 278560 | tf_op jit(solution)/shard_map/ppermute | solution.py:163
  61.5 0.3 take.1
  61.8 38.2 %all_to_all.16.pieces = s16[8,136,128]{2,1,0:T(8,128)(2,1)S(1)} all-to-all(s16[8,136,128]{2,1,0:T(8,128)(2,1)S(1)} %take.1), channel_id=1, replica_groups=mesh['group'=16,'zh'=8,'zl'=2,'core'=2] {'zh'}, dimensions={0} | all-to-all | bytes 557056 | tf_op jit(solution)/shard_map/all_to_all | solution.py:165
  99.9 0.7 finish.1
  (6 shorter events, 0.1 us)
Async XLA Ops:
  1.4 15.3 %all-to-all-start = ((s32[16,1,4]{2,1,0:T(1,128)}), s32[16,1,4]{2,1,0:T(1,128)S(1)}, u32[]{:S(2)}, u32[]{:S(2)}) async-start(s32[16,1,4]{2,1,0:T(1,128)} %copy.7), calls=%async_computation | async-start | bytes 16384 | tf_op jit(solution)/shard_map/all_to_all | solution.py:175
  48.3 4.6 %collective-permute-start = (f32[16,128,128]{2,1,0:T(8,128)S(1)}, f32[16,128,128]{2,1,0:T(8,128)S(1)}, u32[]{:S(2)}, u32[]{:S(2)}) collective-permute-start(f32[16,128,128]{2,1,0:T(8,128)S(1)} %contract_0.1), channel_id=1, source_target_pairs={{0,1},{1,0},{2,3},{3,2},{4,5},{5,4},{6,7},{7,6},{8,9},{9,8},{10,11... | collective-permute-start | bytes 3145736 | tf_op jit(solution)/shard_map/ppermute | solution.py:185
  53.1 8.4 %collective-permute-start.1 = (s16[8,136,128]{2,1,0:T(8,128)(2,1)S(1)}, s16[8,136,128]{2,1,0:T(8,128)(2,1)S(1)}, u32[]{:S(2)}, u32[]{:S(2)}) collective-permute-start(s16[8,136,128]{2,1,0:T(8,128)(2,1)S(1)} %give.1), channel_id=1, source_target_pairs={{0,2},{1,31},{2,0},{3,5},{4,6},{5,3},{6,4},{7,9},{8,10},{9,7},{10,... | collective-permute-start | bytes 835592 | tf_op jit(solution)/shard_map/ppermute | solution.py:163

commit v7 on v6

--- a/solution.py
+++ b/solution.py
@@ -11,7 +11,7 @@
 GROUP_MEMBER = ("group", "zh", "zl", "core")
 Z = ("zh", "zl")
 PAIR = 2
-UNROLL = 24
+UNROLL = 16
 SLOTS = 512
 TOP = 32760.0
 SCALE_ROWS = 8
@@ -49,7 +49,7 @@
     half = tiles // 2
     k = jnp.arange(tasks.shape[0], dtype=jnp.int32)
     valid = k < counts[0]
-    side = ((r & 1) ^ core ^ 1) * half + (((r >> 1) & 1) ^ parity ^ 1) * (half // 2) + (r >> 2)
+    side = (((r >> 1) & 1) ^ parity ^ 1) * half + ((r & 1) ^ core ^ 1) * (half // 2) + (r >> 2)
     q = jnp.where(valid, side, tiles)
     code = a + s * 32
     rank = jnp.sum(((q[:, None] == q[None, :]) & (k[None, :] < k[:, None])).astype(jnp.int32), 1)
@@ -66,9 +66,9 @@
     return table, target, ends
 
 
-def contract_kernel(which, half, blank, table, target, ends, amps, fetched, out):
-    low = ends[half - 1] if which else 0
-    high = ends[which * half + half - 1]
+def contract_kernel(which, part, blank, table, target, ends, amps, fetched, out):
+    low = ends[which * part - 1] if which else 0
+    high = ends[which * part + part - 1]
     out[...] = jnp.zeros_like(out)
 
     def step(i, carry):
@@ -81,27 +81,27 @@
             products.append(jnp.dot(left, right, preferred_element_type=jnp.float32))
         for u in range(UNROLL):
             j = low + i * UNROLL + u
-            out[jnp.minimum(target[j] - which * half, half - 1)] += products[u]
+            out[jnp.minimum(target[j] - which * part, part - 1)] += products[u]
         return carry
 
     lax.fori_loop(0, (high - low + UNROLL - 1) // UNROLL, step, 0)
 
 
-def contract(which, tables, amps, fetched, half, blank):
+def contract(which, tables, amps, fetched, part, blank):
     size = amps.shape[1]
     full = lambda n: pl.BlockSpec((n, size, size), lambda i, *_: (0, 0, 0))
     return pl.pallas_call(
-        functools.partial(contract_kernel, which, half, blank),
+        functools.partial(contract_kernel, which, part, blank),
         grid_spec=pltpu.PrefetchScalarGridSpec(
             num_scalar_prefetch=3,
             grid=(1,),
             in_specs=[full(amps.shape[0]), full(fetched.shape[0])],
-            out_specs=full(half),
+            out_specs=full(part),
         ),
-        out_shape=jax.ShapeDtypeStruct((half, size, size), jnp.float32),
+        out_shape=jax.ShapeDtypeStruct((part, size, size), jnp.float32),
         compiler_params=pltpu.CompilerParams(vmem_limit_bytes=16 << 20),
         cost_estimate=pl.CostEstimate(
-            flops=1 << 32, bytes_accessed=4 << 20, transcendentals=0
+            flops=1 << 31, bytes_accessed=3 << 20, transcendentals=0
         ),
         name="contract_%d" % which,
     )(*tables, amps, fetched)
@@ -141,8 +141,7 @@
 
 def take_kernel(own, other, arrived, out):
     for i in range(out.shape[0]):
-        k = out.shape[0] + i
-        store_coded(own[k] + other[k] + load_coded(arrived, i), out, i)
+        store_coded(own[i] + other[i] + load_coded(arrived, i), out, i)
 
 
 def finish_kernel(pieces, out):
@@ -152,20 +151,12 @@
     out[0] = total
 
 
-def reduce_members(own, other):
-    tiles, size, _ = own.shape
-    coded = jax.ShapeDtypeStruct((tiles // 2, size + SCALE_ROWS, size), jnp.int16)
-    arrived = plain_call(give_kernel, "give", coded, own, other)
+def near_route(chips):
     route = []
-    for z in range(tiles):
+    for z in range(chips):
         route.append((2 * z, 2 * (z ^ 1)))
-        route.append((2 * z + 1, 2 * ((z + 1 if z % 2 else z - 1) % tiles) + 1))
-    arrived = lax.ppermute(arrived, (*Z, "core"), route)
-    pieces = plain_call(take_kernel, "take", coded, own, other, arrived)
-    pieces = lax.all_to_all(pieces, "zh", split_axis=0, concat_axis=0, tiled=True)
-    return plain_call(
-        finish_kernel, "finish", jax.ShapeDtypeStruct((1, size, size), jnp.float32), pieces
-    )
+        route.append((2 * z + 1, 2 * ((z + 1 if z % 2 else z - 1) % chips) + 1))
+    return route
 
 
 def per_device(amplitudes, integrals, tasks, requests, counts):
@@ -181,10 +172,20 @@
     fetched = lax.all_to_all(
         select(wanted, local, amount + 1), "group", split_axis=0, concat_axis=0, tiled=True
     )
-    other = contract(0, tables, local, fetched, half, amount)
-    other = lax.ppermute(other, "core", [(0, 1), (1, 0)])
-    own = contract(1, tables, local, fetched, half, amount)
-    return reduce_members(own, other)
+    part = half // 2
+    tiles = lambda which, tables: contract(which, tables, local, fetched, part, amount)
+    swap = lambda x: lax.ppermute(x, "core", [(0, 1), (1, 0)])
+    coded = jax.ShapeDtypeStruct((part, tile + SCALE_ROWS, tile), jnp.int16)
+
+    other = swap(tiles(0, tables))
+    away = plain_call(give_kernel, "give", coded, tiles(1, tables), other)
+    away, tables = lax.optimization_barrier((away, tables))
+    arrived = lax.ppermute(away, (*Z, "core"), near_route(half))
+    other = swap(tiles(2, tables))
+    pieces = plain_call(take_kernel, "take", coded, tiles(3, tables), other, arrived)
+    pieces = lax.all_to_all(pieces, "zh", split_axis=0, concat_axis=0, tiled=True)
+    total = jax.ShapeDtypeStruct((1, tile, tile), jnp.float32)
+    return plain_call(finish_kernel, "finish", total, pieces)
 
 
 def solution(mesh):

time: 101 us -> 105 us (1.040)
  the two profiles are of different devices: /device:TPU:2 before, /device:TPU:1 now
where the time goes in v7:
time: 105 us
  blocking collectives  59 us (56%)
  starting transfers between devices  28.4 us (27%)
  Pallas kernels  6.32 us (6%)
  waiting for transfers between devices  5.87 us (6%)
  other arithmetic  2.95 us (3%)
  local copies, waits for them, and re-layouts  1.43 us (1%)
    all_to_all x1, blocking collectives, per_device(): lax.all_to_all(pieces, 'zh', split_axis=0, concat_axis=0, tiled=True)  30.1 us
    all_to_all x1, blocking collectives, per_device(): lax.all_to_all(select(wanted, local, amount + 1), 'group', split_axis=0,...  28.8 us
    ppermute x1, starting transfers between devices, per_device(): arrived = lax.ppermute(away, (*Z, 'core'), near_route(half))  11.8 us
    ppermute x2, starting transfers between devices, per_device(): swap = lambda x: lax.ppermute(x, 'core', [(0, 1), (1, 0)])  9.05 us
    all_to_all x1, starting transfers between devices, per_device(): lax.all_to_all(asked, 'group', split_axis=0, concat_axis=0, tiled=True)  7.58 us
    pallas_call x4, Pallas kernels, contract(): pl.pallas_call(functools.partial(contract_kernel, which, part, blank), gr...  4.34 us
    ppermute x1, waiting for transfers between devices, per_device(): arrived = lax.ppermute(away, (*Z, 'core'), near_route(half))  2.83 us
    all_to_all x1, waiting for transfers between devices, per_device(): lax.all_to_all(asked, 'group', split_axis=0, concat_axis=0, tiled=True)  2.62 us
  transfers between devices with their start and end apart: 4, of which 3 were waited for; matrix products, arithmetic and copies ran while one was open for 3% of the time, Pallas kernels for 2%

profile of v7, /device:TPU:1, one launch (start us, length us, event | category | flops | bytes accessed | tf_op | source)
XLA Modules:
  0.0 104.7 jit_solution(7078031817977941972)
XLA Ops:
  0.0 1.4 %copy.7 = s32[16,1,4]{2,1,0:T(1,128)} copy(s32[16,1,4]{0,2,1:T(4,128)} %bitcast.8) | data formatting | bytes 512 | tf_op jit(solution)/shard_map/reshape | solution.py:165
  1.4 7.6 %all-to-all-start = ((s32[16,1,4]{2,1,0:T(1,128)}), s32[16,1,4]{2,1,0:T(1,128)S(1)}, u32[]{:S(2)}, u32[]{:S(2)}) async-start(s32[16,1,4]{2,1,0:T(1,128)} %copy.7), calls=%async_computation | async-start | bytes 16384 | tf_op jit(solution)/shard_map/all_to_all | solution.py:166
  9.6 0.8 add_add_fusion
  10.5 0.1 convert_reduce_fusion.1
  10.6 0.2 convert_reduce_fusion
  10.8 0.1 select_reduce_fusion.2.ends
  10.9 0.1 select_reduce_fusion.1
  11.0 0.2 select_reduce_fusion
  11.2 0.1 pad.1.clone
  11.3 1.3 %pad_maximum_fusion.local.amps = bf16[25,128,128]{2,1,0:T(8,128)(2,1)S(1)} fusion(bf16[8,128,128]{2,1,0:T(8,128)(2,1)} %param.6, bf16[16,128,128]{2,1,0:T(8,128)(2,1)} %param.5, bf16[25]{0:T(256)(128)(2,1)S(1)} %pad.1.clone), kind=kLoop, calls=%fused_computation | loop fusion | flops 819200 | bytes 1605682 | tf_op jit(solution)/shard_map/concatenate | solution.py:170
  12.6 0.1 convert_reduce_fusion.2.target
  12.7 2.6 %all-to-all-done.wanted = s32[16,1,4]{2,1,0:T(1,128)S(1)} async-done(((s32[16,1,4]{2,1,0:T(1,128)}), s32[16,1,4]{2,1,0:T(1,128)S(1)}, u32[]{:S(2)}, u32[]{:S(2)}) %all-to-all-start) | async-done | bytes 288 | tf_op jit(solution)/shard_map/all_to_all | solution.py:166
  15.3 0.8 select.31
  16.1 28.8 %all_to_all.15.fetched = bf16[64,128,128]{2,1,0:T(8,128)(2,1)S(1)} all-to-all(bf16[64,128,128]{2,1,0:T(8,128)(2,1)S(1)} %select.31), channel_id=1, replica_groups=mesh['group'=16,'zh'=8,'zl'=2,'core'=2] {'group'}, dimensions={0} | all-to-all | bytes 4194304 | tf_op jit(solution)/shard_map/all_to_all | solution.py:172
  44.9 1.1 %contract_0.1 = f32[8,128,128]{2,1,0:T(8,128)S(1)} custom-call(s32[512]{0:T(512)S(1)} %broadcast_add_fusion.table, s32[256]{0:T(256)S(1)} %convert_reduce_fusion.2.target, s32[32]{0:T(128)S(1)} %select_reduce_fusion.2.ends, bf16[25,128,128]{2,1,0:T(8,128)(2,1)S(1)} %pad_maximum_fusion.local.amps, bf16[64,128,128]{2,1,0:T(8,128)(2,1)S(1)} %all_to_all.15.fetched), custom_call_target="tpu_custom_call" | custom-call | flops 2147483648 | bytes 3145728 | tf_op jit(solution)/shard_map/contract_0/pallas_call | solution.py:93
  46.0 6.3 %collective-permute-start = (f32[8,128,128]{2,1,0:T(8,128)S(1)}, f32[8,128,128]{2,1,0:T(8,128)S(1)}, u32[]{:S(2)}, u32[]{:S(2)}) collective-permute-start(f32[8,128,128]{2,1,0:T(8,128)S(1)} %contract_0.1), channel_id=1, source_target_pairs={{0,1},{1,0},{2,3},{3,2},{4,5},{5,4},{6,7},{7,6},{8,9},{9,8},{10,11... | collective-permute-start | bytes 1572872 | tf_op jit(solution)/shard_map/ppermute | solution.py:177
  52.3 1.1 %contract_1.1.own = f32[8,128,128]{2,1,0:T(8,128)S(1)} custom-call(s32[512]{0:T(512)S(1)} %broadcast_add_fusion.table, s32[256]{0:T(256)S(1)} %convert_reduce_fusion.2.target, s32[32]{0:T(128)S(1)} %select_reduce_fusion.2.ends, bf16[25,128,128]{2,1,0:T(8,128)(2,1)S(1)} %pad_maximum_fusion.local.amps, bf16[64,128,128]{2,1,0:T(8,128)(2,1)S(1)} %all_to_all.15.fetched), custom_call_target="tpu_custom_call" | custom-call | flops 2147483648 | bytes 3145728 | tf_op jit(solution)/shard_map/contract_1/pallas_call | solution.py:93
  53.4 0.4 collective-permute-done.other
  53.8 0.2 give.1
  54.1 1.1 %contract_2.1 = f32[8,128,128]{2,1,0:T(8,128)S(1)} custom-call(s32[512]{0:T(512)S(1)} %broadcast_add_fusion.table, s32[256]{0:T(256)S(1)} %convert_reduce_fusion.2.target, s32[32]{0:T(128)S(1)} %select_reduce_fusion.2.ends, bf16[25,128,128]{2,1,0:T(8,128)(2,1)S(1)} %pad_maximum_fusion.local.amps, bf16[64,128,128]{2,1,0:T(8,128)(2,1)S(1)} %all_to_all.15.fetched), custom_call_target="tpu_custom_call" | custom-call | flops 2147483648 | bytes 3145728 | tf_op jit(solution)/shard_map/contract_2/pallas_call | solution.py:93
  55.1 2.7 %collective-permute-start.1 = (f32[8,128,128]{2,1,0:T(8,128)S(1)}, f32[8,128,128]{2,1,0:T(8,128)S(1)}, u32[]{:S(2)}, u32[]{:S(2)}) collective-permute-start(f32[8,128,128]{2,1,0:T(8,128)S(1)} %contract_2.1), channel_id=1, source_target_pairs={{0,1},{1,0},{2,3},{3,2},{4,5},{5,4},{6,7},{7,6},{8,9},{9,8},{10,11... | collective-permute-start | bytes 1572872 | tf_op jit(solution)/shard_map/ppermute | solution.py:177
  57.9 11.8 %collective-permute-start.2 = (s16[8,136,128]{2,1,0:T(8,128)(2,1)S(1)}, s16[8,136,128]{2,1,0:T(8,128)(2,1)S(1)}, u32[]{:S(2)}, u32[]{:S(2)}) collective-permute-start(s16[8,136,128]{2,1,0:T(8,128)(2,1)S(1)} %give.1), channel_id=1, source_target_pairs={{0,2},{1,31},{2,0},{3,5},{4,6},{5,3},{6,4},{7,9},{8,10},{9,7},{10,... | collective-permute-start | bytes 835592 | tf_op jit(solution)/shard_map/ppermute | solution.py:183
  69.7 1.1 %contract_3.1.own = f32[8,128,128]{2,1,0:T(8,128)S(1)} custom-call(s32[512]{0:T(512)S(1)} %broadcast_add_fusion.table, s32[256]{0:T(256)S(1)} %convert_reduce_fusion.2.target, s32[32]{0:T(128)S(1)} %select_reduce_fusion.2.ends, bf16[25,128,128]{2,1,0:T(8,128)(2,1)S(1)} %pad_maximum_fusion.local.amps, bf16[64,128,128]{2,1,0:T(8,128)(2,1)S(1)} %all_to_all.15.fetched), custom_call_target="tpu_custom_call" | custom-call | flops 2147483648 | bytes 3145728 | tf_op jit(solution)/shard_map/contract_3/pallas_call | solution.py:93
  70.8 2.8 %collective-permute-done.2.arrived = s16[8,136,128]{2,1,0:T(8,128)(2,1)S(1)} collective-permute-done((s16[8,136,128]{2,1,0:T(8,128)(2,1)S(1)}, s16[8,136,128]{2,1,0:T(8,128)(2,1)S(1)}, u32[]{:S(2)}, u32[]{:S(2)}) %collective-permute-start.2) | collective-permute-done | bytes 278560 | tf_op jit(solution)/shard_map/ppermute | solution.py:183
  73.6 0.0 collective-permute-done.1.other
  73.6 0.3 take.1
  73.9 30.1 %all_to_all.16.pieces = s16[8,136,128]{2,1,0:T(8,128)(2,1)S(1)} all-to-all(s16[8,136,128]{2,1,0:T(8,128)(2,1)S(1)} %take.1), channel_id=1, replica_groups=mesh['group'=16,'zh'=8,'zl'=2,'core'=2] {'zh'}, dimensions={0} | all-to-all | bytes 557056 | tf_op jit(solution)/shard_map/all_to_all | solution.py:186
  104.0 0.7 finish.1
  (6 shorter events, 0.1 us)
Async XLA Ops:
  1.4 13.9 %all-to-all-start = ((s32[16,1,4]{2,1,0:T(1,128)}), s32[16,1,4]{2,1,0:T(1,128)S(1)}, u32[]{:S(2)}, u32[]{:S(2)}) async-start(s32[16,1,4]{2,1,0:T(1,128)} %copy.7), calls=%async_computation | async-start | bytes 16384 | tf_op jit(solution)/shard_map/all_to_all | solution.py:166
  46.0 7.8 %collective-permute-start = (f32[8,128,128]{2,1,0:T(8,128)S(1)}, f32[8,128,128]{2,1,0:T(8,128)S(1)}, u32[]{:S(2)}, u32[]{:S(2)}) collective-permute-start(f32[8,128,128]{2,1,0:T(8,128)S(1)} %contract_0.1), channel_id=1, source_target_pairs={{0,1},{1,0},{2,3},{3,2},{4,5},{5,4},{6,7},{7,6},{8,9},{9,8},{10,11... | collective-permute-start | bytes 1572872 | tf_op jit(solution)/shard_map/ppermute | solution.py:177
  55.1 18.5 %collective-permute-start.1 = (f32[8,128,128]{2,1,0:T(8,128)S(1)}, f32[8,128,128]{2,1,0:T(8,128)S(1)}, u32[]{:S(2)}, u32[]{:S(2)}) collective-permute-start(f32[8,128,128]{2,1,0:T(8,128)S(1)} %contract_2.1), channel_id=1, source_target_pairs={{0,1},{1,0},{2,3},{3,2},{4,5},{5,4},{6,7},{7,6},{8,9},{9,8},{10,11... | collective-permute-start | bytes 1572872 | tf_op jit(solution)/shard_map/ppermute | solution.py:177
  57.9 15.7 %collective-permute-start.2 = (s16[8,136,128]{2,1,0:T(8,128)(2,1)S(1)}, s16[8,136,128]{2,1,0:T(8,128)(2,1)S(1)}, u32[]{:S(2)}, u32[]{:S(2)}) collective-permute-start(s16[8,136,128]{2,1,0:T(8,128)(2,1)S(1)} %give.1), channel_id=1, source_target_pairs={{0,2},{1,31},{2,0},{3,5},{4,6},{5,3},{6,4},{7,9},{8,10},{9,7},{10,... | collective-permute-start | bytes 835592 | tf_op jit(solution)/shard_map/ppermute | solution.py:183

commit v8 on v6

--- a/solution.py
+++ b/solution.py
@@ -177,7 +177,7 @@
     tables = task_tables(tasks, counts, core, parity, 2 * half, amount)
     blank = jnp.zeros((1, tile, tile), amplitudes.dtype)
     local = jnp.concatenate([amplitudes, blank, integrals])
-    wanted, tables, local = lax.optimization_barrier((wanted, tables, local))
+    wanted, local = lax.optimization_barrier((wanted, local))
     fetched = lax.all_to_all(
         select(wanted, local, amount + 1), "group", split_axis=0, concat_axis=0, tiled=True
     )

time: 101 us -> 106 us (1.050)
  the two profiles are of different devices: /device:TPU:2 before, /device:TPU:1 now
where the time goes in v8:
time: 106 us; the launch traced here: 105 us
  waiting for transfers between devices  32.1 us (30%)
  blocking collectives  30.4 us (29%)
  starting transfers between devices  28.5 us (27%)
  Pallas kernels  10.1 us (10%)
  other arithmetic  2.15 us (2%)
  local copies, waits for them, and re-layouts  1.43 us (1%)
    all_to_all x1, blocking collectives, reduce_members(): lax.all_to_all(pieces, 'zh', split_axis=0, concat_axis=0, tiled=True)  30.4 us
    all_to_all x1, waiting for transfers between devices, per_device(): lax.all_to_all(select(wanted, local, amount + 1), 'group', split_axis=0,...  23.1 us
    ppermute x1, starting transfers between devices, reduce_members(): arrived = lax.ppermute(arrived, (*Z, 'core'), route)  9.02 us
    ppermute x1, starting transfers between devices, per_device(): other = lax.ppermute(other, 'core', [(0, 1), (1, 0)])  8.02 us
    all_to_all x1, starting transfers between devices, per_device(): lax.all_to_all(asked, 'group', split_axis=0, concat_axis=0, tiled=True)  7.58 us
    pallas_call x2, Pallas kernels, contract(): pl.pallas_call(functools.partial(contract_kernel, which, half, blank), gr...  6.83 us
    all_to_all x1, waiting for transfers between devices, per_device(): lax.all_to_all(asked, 'group', split_axis=0, concat_axis=0, tiled=True)  4.98 us
    ppermute x1, waiting for transfers between devices, reduce_members(): arrived = lax.ppermute(arrived, (*Z, 'core'), route)  3.92 us
  transfers between devices with their start and end apart: 4, of which 3 were waited for; matrix products, arithmetic and copies ran while one was open for 2% of the time, Pallas kernels for 4%

profile of v8, /device:TPU:1, one launch (start us, length us, event | category | flops | bytes accessed | tf_op | source)
XLA Modules:
  0.0 105.5 jit_solution(2017824438687132799)
XLA Ops:
  0.0 1.4 %copy.7 = s32[16,1,4]{2,1,0:T(1,128)} copy(s32[16,1,4]{0,2,1:T(4,128)} %bitcast.8) | data formatting | bytes 512 | tf_op jit(solution)/shard_map/reshape | solution.py:174
  1.4 7.6 %all-to-all-start = ((s32[16,1,4]{2,1,0:T(1,128)}), s32[16,1,4]{2,1,0:T(1,128)S(1)}, u32[]{:S(2)}, u32[]{:S(2)}) async-start(s32[16,1,4]{2,1,0:T(1,128)} %copy.7), calls=%async_computation | async-start | bytes 16384 | tf_op jit(solution)/shard_map/all_to_all | solution.py:175
  9.0 0.1 pad.1.clone
  9.0 1.3 %pad_maximum_fusion.local.amps = bf16[25,128,128]{2,1,0:T(8,128)(2,1)S(1)} fusion(bf16[8,128,128]{2,1,0:T(8,128)(2,1)} %param.6, bf16[16,128,128]{2,1,0:T(8,128)(2,1)} %param.5, bf16[25]{0:T(256)(128)(2,1)S(1)} %pad.1.clone), kind=kLoop, calls=%fused_computation | loop fusion | flops 819200 | bytes 1605682 | tf_op jit(solution)/shard_map/concatenate | solution.py:179
  10.3 5.0 %all-to-all-done.wanted = s32[16,1,4]{2,1,0:T(1,128)S(1)} async-done(((s32[16,1,4]{2,1,0:T(1,128)}), s32[16,1,4]{2,1,0:T(1,128)S(1)}, u32[]{:S(2)}, u32[]{:S(2)}) %all-to-all-start) | async-done | bytes 288 | tf_op jit(solution)/shard_map/all_to_all | solution.py:175
  15.3 2.2 %select.31 = bf16[64,128,128]{2,1,0:T(8,128)(2,1)} custom-call(s32[16,1,4]{2,1,0:T(1,128)S(1)} %all-to-all-done.wanted, bf16[25,128,128]{2,1,0:T(8,128)(2,1)S(1)} %pad_maximum_fusion.local.amps), custom_call_target="tpu_custom_call" | custom-call | bytes 2097152 | tf_op jit(solution)/shard_map/select/pallas_call | solution.py:32
  17.4 0.0 copy-start
  17.4 3.8 %all-to-all-start.1 = ((bf16[64,128,128]{2,1,0:T(8,128)(2,1)}), bf16[64,128,128]{2,1,0:T(8,128)(2,1)S(1)}, u32[]{:S(2)}, u32[]{:S(2)}) async-start(bf16[64,128,128]{2,1,0:T(8,128)(2,1)} %select.31), calls=%async_computation.1 | async-start | bytes 4194304 | tf_op jit(solution)/shard_map/all_to_all | solution.py:181
  21.3 0.0 copy-done
  22.0 0.1 convert_reduce_fusion.1
  22.2 0.1 select_reduce_fusion.2.ends
  22.2 0.1 convert_reduce_fusion.2.target
  22.4 0.1 select_reduce_fusion.1
  22.4 0.2 convert_reduce_fusion
  22.7 0.2 select_reduce_fusion
  22.9 23.1 %all-to-all-done.1.fetched = bf16[64,128,128]{2,1,0:T(8,128)(2,1)S(1)} async-done(((bf16[64,128,128]{2,1,0:T(8,128)(2,1)}), bf16[64,128,128]{2,1,0:T(8,128)(2,1)S(1)}, u32[]{:S(2)}, u32[]{:S(2)}) %all-to-all-start.1) | async-done | bytes 2097184 | tf_op jit(solution)/shard_map/all_to_all | solution.py:181
  46.0 3.1 %contract_0.1 = f32[16,128,128]{2,1,0:T(8,128)S(1)} custom-call(s32[512]{0:T(512)S(1)} %broadcast_add_fusion.table, s32[256]{0:T(256)S(1)} %convert_reduce_fusion.2.target, s32[32]{0:T(128)S(1)} %select_reduce_fusion.2.ends, bf16[25,128,128]{2,1,0:T(8,128)(2,1)S(1)} %pad_maximum_fusion.local.amps, bf16[64,128,128]{2,1,0:T(8,128)(2,1)S(1)} %all-to-all-done.1.fetched), custom_call_target="tpu_custom_call" | custom-call | flops 4294967296 | bytes 4194304 | tf_op jit(solution)/shard_map/contract_0/pallas_call | solution.py:93
  49.1 8.0 %collective-permute-start = (f32[16,128,128]{2,1,0:T(8,128)S(1)}, f32[16,128,128]{2,1,0:T(8,128)S(1)}, u32[]{:S(2)}, u32[]{:S(2)}) collective-permute-start(f32[16,128,128]{2,1,0:T(8,128)S(1)} %contract_0.1), channel_id=1, source_target_pairs={{0,1},{1,0},{2,3},{3,2},{4,5},{5,4},{6,7},{7,6},{8,9},{9,8},{10,11... | collective-permute-start | bytes 3145736 | tf_op jit(solution)/shard_map/ppermute | solution.py:185
  57.2 3.7 %contract_1.1.own = f32[16,128,128]{2,1,0:T(8,128)S(1)} custom-call(s32[512]{0:T(512)S(1)} %broadcast_add_fusion.table, s32[256]{0:T(256)S(1)} %convert_reduce_fusion.2.target, s32[32]{0:T(128)S(1)} %select_reduce_fusion.2.ends, bf16[25,128,128]{2,1,0:T(8,128)(2,1)S(1)} %pad_maximum_fusion.local.amps, bf16[64,128,128]{2,1,0:T(8,128)(2,1)S(1)} %all-to-all-done.1.fetched), custom_call_target="tpu_custom_call" | custom-call | flops 4294967296 | bytes 4194304 | tf_op jit(solution)/shard_map/contract_1/pallas_call | solution.py:93
  60.9 0.0 collective-permute-done.other
  60.9 0.2 give.1
  61.1 9.0 %collective-permute-start.1 = (s16[8,136,128]{2,1,0:T(8,128)(2,1)S(1)}, s16[8,136,128]{2,1,0:T(8,128)(2,1)S(1)}, u32[]{:S(2)}, u32[]{:S(2)}) collective-permute-start(s16[8,136,128]{2,1,0:T(8,128)(2,1)S(1)} %give.1), channel_id=1, source_target_pairs={{0,2},{1,31},{2,0},{3,5},{4,6},{5,3},{6,4},{7,9},{8,10},{9,7},{10,... | collective-permute-start | bytes 835592 | tf_op jit(solution)/shard_map/ppermute | solution.py:163
  70.1 3.9 %collective-permute-done.1.arrived = s16[8,136,128]{2,1,0:T(8,128)(2,1)S(1)} collective-permute-done((s16[8,136,128]{2,1,0:T(8,128)(2,1)S(1)}, s16[8,136,128]{2,1,0:T(8,128)(2,1)S(1)}, u32[]{:S(2)}, u32[]{:S(2)}) %collective-permute-start.1) | collective-permute-done | bytes 278560 | tf_op jit(solution)/shard_map/ppermute | solution.py:163
  74.1 0.3 take.1
  74.3 30.4 %all_to_all.15.pieces = s16[8,136,128]{2,1,0:T(8,128)(2,1)S(1)} all-to-all(s16[8,136,128]{2,1,0:T(8,128)(2,1)S(1)} %take.1), channel_id=1, replica_groups=mesh['group'=16,'zh'=8,'zl'=2,'core'=2] {'zh'}, dimensions={0} | all-to-all | bytes 557056 | tf_op jit(solution)/shard_map/all_to_all | solution.py:165
  104.8 0.7 finish.1
  (7 shorter events, 0.1 us)
Async XLA Ops:
  1.4 13.9 %all-to-all-start = ((s32[16,1,4]{2,1,0:T(1,128)}), s32[16,1,4]{2,1,0:T(1,128)S(1)}, u32[]{:S(2)}, u32[]{:S(2)}) async-start(s32[16,1,4]{2,1,0:T(1,128)} %copy.7), calls=%async_computation | async-start | bytes 16384 | tf_op jit(solution)/shard_map/all_to_all | solution.py:175
  17.4 3.9 %copy-start = (s32[384,3]{0,1:T(4,128)S(1)}, s32[384,3]{0,1:T(4,128)}, u32[]{:S(2)}) copy-start(s32[384,3]{0,1:T(4,128)} %param.7) | copy-start | bytes 13828
  17.4 28.6 %all-to-all-start.1 = ((bf16[64,128,128]{2,1,0:T(8,128)(2,1)}), bf16[64,128,128]{2,1,0:T(8,128)(2,1)S(1)}, u32[]{:S(2)}, u32[]{:S(2)}) async-start(bf16[64,128,128]{2,1,0:T(8,128)(2,1)} %select.31), calls=%async_computation.1 | async-start | bytes 4194304 | tf_op jit(solution)/shard_map/all_to_all | solution.py:181
  49.1 11.8 %collective-permute-start = (f32[16,128,128]{2,1,0:T(8,128)S(1)}, f32[16,128,128]{2,1,0:T(8,128)S(1)}, u32[]{:S(2)}, u32[]{:S(2)}) collective-permute-start(f32[16,128,128]{2,1,0:T(8,128)S(1)} %contract_0.1), channel_id=1, source_target_pairs={{0,1},{1,0},{2,3},{3,2},{4,5},{5,4},{6,7},{7,6},{8,9},{9,8},{10,11... | collective-permute-start | bytes 3145736 | tf_op jit(solution)/shard_map/ppermute | solution.py:185
  61.1 13.0 %collective-permute-start.1 = (s16[8,136,128]{2,1,0:T(8,128)(2,1)S(1)}, s16[8,136,128]{2,1,0:T(8,128)(2,1)S(1)}, u32[]{:S(2)}, u32[]{:S(2)}) collective-permute-start(s16[8,136,128]{2,1,0:T(8,128)(2,1)S(1)} %give.1), channel_id=1, source_target_pairs={{0,2},{1,31},{2,0},{3,5},{4,6},{5,3},{6,4},{7,9},{8,10},{9,7},{10,... | collective-permute-start | bytes 835592 | tf_op jit(solution)/shard_map/ppermute | solution.py:163

commit v9 on v7

--- a/solution.py
+++ b/solution.py
@@ -11,28 +11,28 @@
 GROUP_MEMBER = ("group", "zh", "zl", "core")
 Z = ("zh", "zl")
 PAIR = 2
-UNROLL = 16
+
 SLOTS = 512
 TOP = 32760.0
 SCALE_ROWS = 8
 STEPS = 128.0
 
 
-def select_kernel(base, wanted, local, out):
-    rows, _, cap = wanted.shape
+def select_kernel(base, me, wanted, local, out):
+    rows, cap, _ = wanted.shape
     for i in range(rows):
         for c in range(cap):
-            out[i * cap + c] = local[base + wanted[i, 0, c]]
-
-
-def select(wanted, local, base):
+            out[i * cap + c] = local[base + wanted[i, c, me[0]]]
+
+
+def select(me, wanted, local, base):
     size = local.shape[1]
-    slots = wanted.shape[0] * wanted.shape[2]
+    slots = wanted.shape[0] * wanted.shape[1]
     full = lambda n: pl.BlockSpec((n, size, size), lambda i, *_: (0, 0, 0))
     return pl.pallas_call(
         functools.partial(select_kernel, base),
         grid_spec=pltpu.PrefetchScalarGridSpec(
-            num_scalar_prefetch=1,
+            num_scalar_prefetch=2,
             grid=(1,),
             in_specs=[full(local.shape[0])],
             out_specs=full(slots),
@@ -41,7 +41,7 @@
         compiler_params=pltpu.CompilerParams(vmem_limit_bytes=16 << 20),
         cost_estimate=pl.CostEstimate(flops=0, bytes_accessed=2 << 20, transcendentals=0),
         name="select",
-    )(wanted, local)
+    )(me, wanted, local)
 
 
 def task_tables(tasks, counts, core, parity, tiles, blank):
@@ -49,7 +49,7 @@
     half = tiles // 2
     k = jnp.arange(tasks.shape[0], dtype=jnp.int32)
     valid = k < counts[0]
-    side = (((r >> 1) & 1) ^ parity ^ 1) * half + ((r & 1) ^ core ^ 1) * (half // 2) + (r >> 2)
+    side = ((r & 1) ^ core ^ 1) * half + (((r >> 1) & 1) ^ parity ^ 1) * (half // 2) + (r >> 2)
     q = jnp.where(valid, side, tiles)
     code = a + s * 32
     rank = jnp.sum(((q[:, None] == q[None, :]) & (k[None, :] < k[:, None])).astype(jnp.int32), 1)
@@ -66,44 +66,44 @@
     return table, target, ends
 
 
-def contract_kernel(which, part, blank, table, target, ends, amps, fetched, out):
-    low = ends[which * part - 1] if which else 0
-    high = ends[which * part + part - 1]
+def contract_kernel(first, count, unroll, blank, table, target, ends, amps, fetched, out):
+    low = ends[first - 1] if first else 0
+    high = ends[first + count - 1]
     out[...] = jnp.zeros_like(out)
 
     def step(i, carry):
         products = []
-        for u in range(UNROLL):
-            j = low + i * UNROLL + u
+        for u in range(unroll):
+            j = low + i * unroll + u
             codes = [jnp.where(j < high, table[j * PAIR + n], blank) for n in range(PAIR)]
             left = jnp.concatenate([amps[c & 31] for c in codes], axis=1)
             right = jnp.concatenate([fetched[c >> 5] for c in codes], axis=0)
             products.append(jnp.dot(left, right, preferred_element_type=jnp.float32))
-        for u in range(UNROLL):
-            j = low + i * UNROLL + u
-            out[jnp.minimum(target[j] - which * part, part - 1)] += products[u]
+        for u in range(unroll):
+            j = low + i * unroll + u
+            out[jnp.minimum(target[j] - first, count - 1)] += products[u]
         return carry
 
-    lax.fori_loop(0, (high - low + UNROLL - 1) // UNROLL, step, 0)
-
-
-def contract(which, tables, amps, fetched, part, blank):
+    lax.fori_loop(0, (high - low + unroll - 1) // unroll, step, 0)
+
+
+def contract(first, count, unroll, tables, amps, fetched, blank):
     size = amps.shape[1]
     full = lambda n: pl.BlockSpec((n, size, size), lambda i, *_: (0, 0, 0))
     return pl.pallas_call(
-        functools.partial(contract_kernel, which, part, blank),
+        functools.partial(contract_kernel, first, count, unroll, blank),
         grid_spec=pltpu.PrefetchScalarGridSpec(
             num_scalar_prefetch=3,
             grid=(1,),
             in_specs=[full(amps.shape[0]), full(fetched.shape[0])],
-            out_specs=full(part),
+            out_specs=full(count),
         ),
-        out_shape=jax.ShapeDtypeStruct((part, size, size), jnp.float32),
+        out_shape=jax.ShapeDtypeStruct((count, size, size), jnp.float32),
         compiler_params=pltpu.CompilerParams(vmem_limit_bytes=16 << 20),
         cost_estimate=pl.CostEstimate(
-            flops=1 << 31, bytes_accessed=3 << 20, transcendentals=0
+            flops=1 << 32, bytes_accessed=4 << 20, transcendentals=0
         ),
-        name="contract_%d" % which,
+        name="contract_%d" % first,
     )(*tables, amps, fetched)
 
 
@@ -141,7 +141,8 @@
 
 def take_kernel(own, other, arrived, out):
     for i in range(out.shape[0]):
-        store_coded(own[i] + other[i] + load_coded(arrived, i), out, i)
+        k = out.shape[0] + i
+        store_coded(own[i] + other[k] + load_coded(arrived, i), out, i)
 
 
 def finish_kernel(pieces, out):
@@ -162,7 +163,8 @@
 def per_device(amplitudes, integrals, tasks, requests, counts):
     amount, tile, _ = amplitudes.shape
     half = lax.axis_size(Z)
-    asked = requests.reshape(requests.shape[0], 1, requests.shape[1])
+    asked = jnp.broadcast_to(requests.T, (requests.shape[0], *requests.T.shape))
+    me = lax.axis_index("group").astype(jnp.int32).reshape(1)
     wanted = lax.all_to_all(asked, "group", split_axis=0, concat_axis=0, tiled=True)
     core, parity = lax.axis_index("core"), lax.axis_index("zl")
     tables = task_tables(tasks, counts, core, parity, 2 * half, amount)
@@ -170,19 +172,18 @@
     local = jnp.concatenate([amplitudes, blank, integrals])
     wanted, tables, local = lax.optimization_barrier((wanted, tables, local))
     fetched = lax.all_to_all(
-        select(wanted, local, amount + 1), "group", split_axis=0, concat_axis=0, tiled=True
+        select(me, wanted, local, amount + 1), "group", split_axis=0, concat_axis=0, tiled=True
     )
     part = half // 2
-    tiles = lambda which, tables: contract(which, tables, local, fetched, part, amount)
-    swap = lambda x: lax.ppermute(x, "core", [(0, 1), (1, 0)])
     coded = jax.ShapeDtypeStruct((part, tile + SCALE_ROWS, tile), jnp.int16)
-
-    other = swap(tiles(0, tables))
-    away = plain_call(give_kernel, "give", coded, tiles(1, tables), other)
+    other = contract(0, half, 24, tables, local, fetched, amount)
+    other = lax.ppermute(other, "core", [(0, 1), (1, 0)])
+    own = contract(half, part, 16, tables, local, fetched, amount)
+    away = plain_call(give_kernel, "give", coded, own, other)
     away, tables = lax.optimization_barrier((away, tables))
     arrived = lax.ppermute(away, (*Z, "core"), near_route(half))
-    other = swap(tiles(2, tables))
-    pieces = plain_call(take_kernel, "take", coded, tiles(3, tables), other, arrived)
+    own = contract(half + part, part, 16, tables, local, fetched, amount)
+    pieces = plain_call(take_kernel, "take", coded, own, other, arrived)
     pieces = lax.all_to_all(pieces, "zh", split_axis=0, concat_axis=0, tiled=True)
     total = jax.ShapeDtypeStruct((1, tile, tile), jnp.float32)
     return plain_call(finish_kernel, "finish", total, pieces)

time: 105 us -> 101 us (0.962)
  blocking collectives: 59 us -> 56.2 us
  starting transfers between devices: 28.4 us -> 26.3 us
    ppermute x2 -> x1, starting transfers between devices: 9.05 us -> 6.33 us  [per_device(): other = lax.ppermute(other, 'core', [(0, 1), (1, 0)])]
    all_to_all x1, blocking collectives: 30.1 us -> 27.5 us  [per_device(): lax.all_to_all(pieces, 'zh', split_axis=0, concat_axis=0, tiled=True)]
    reshape x1 -> x0, local copies, waits for them, and re-layouts: 1.35 us -> none  [per_device(): asked = requests.reshape(requests.shape[0], 1, requests.shape[1])]
    broadcast_in_dim x0 -> x1, local copies, waits for them, and re-layouts: none -> 1.3 us  [per_device(): asked = jnp.broadcast_to(requests.T, (requests.shape[0], *requests.T.shape))]
    pallas_call x4 -> x3, Pallas kernels: 4.34 us -> 3.45 us  [contract(): pl.pallas_call(functools.partial(contract_kernel, first, count, unroll, b...]
  transfers between devices with their start and end apart: 4 -> 3, of which waited for: 3 -> 3; matrix products, arithmetic and copies ran while one was open for 3% -> 3% of each run, Pallas kernels for 2% -> 2%
where the time goes in v9:
time: 101 us; the launch traced here: 100 us
  blocking collectives  56.2 us (56%)
  starting transfers between devices  26.3 us (26%)
  waiting for transfers between devices  6.73 us (7%)
  Pallas kernels  5.83 us (6%)
  other arithmetic  2.96 us (3%)
  local copies, waits for them, and re-layouts  1.38 us (1%)
    all_to_all x1, blocking collectives, per_device(): lax.all_to_all(select(me, wanted, local, amount + 1), 'group', split_axis...  28.7 us
    all_to_all x1, blocking collectives, per_device(): lax.all_to_all(pieces, 'zh', split_axis=0, concat_axis=0, tiled=True)  27.5 us
    ppermute x1, starting transfers between devices, per_device(): arrived = lax.ppermute(away, (*Z, 'core'), near_route(half))  12.4 us
    all_to_all x1, starting transfers between devices, per_device(): lax.all_to_all(asked, 'group', split_axis=0, concat_axis=0, tiled=True)  7.58 us
    ppermute x1, starting transfers between devices, per_device(): other = lax.ppermute(other, 'core', [(0, 1), (1, 0)])  6.33 us
    pallas_call x3, Pallas kernels, contract(): pl.pallas_call(functools.partial(contract_kernel, first, count, unroll, b...  3.45 us
    ppermute x1, waiting for transfers between devices, per_device(): arrived = lax.ppermute(away, (*Z, 'core'), near_route(half))  2.83 us
    all_to_all x1, waiting for transfers between devices, per_device(): lax.all_to_all(asked, 'group', split_axis=0, concat_axis=0, tiled=True)  2.74 us
  transfers between devices with their start and end apart: 3, of which 3 were waited for; matrix products, arithmetic and copies ran while one was open for 3% of the time, Pallas kernels for 2%

profile of v9, /device:TPU:1, one launch (start us, length us, event | category | flops | bytes accessed | tf_op | source)
XLA Modules:
  0.0 100.1 jit_solution(17916419322193591788)
XLA Ops:
  0.0 1.3 %broadcast_in_dim.66 = s32[16,4,16]{2,1,0:T(4,128)} broadcast(s32[4,16]{1,0:T(4,128)} %bitcast.9), dimensions={1,2} | broadcast | bytes 4352 | tf_op jit(solution)/shard_map/broadcast_in_dim | solution.py:166
  1.3 7.6 %all-to-all-start = ((s32[16,4,16]{2,1,0:T(4,128)}), s32[16,4,16]{2,1,0:T(4,128)S(1)}, u32[]{:S(2)}, u32[]{:S(2)}) async-start(s32[16,4,16]{2,1,0:T(4,128)} %broadcast_in_dim.66), calls=%async_computation | async-start | bytes 65536 | tf_op jit(solution)/shard_map/all_to_all | solution.py:168
  9.5 0.8 add_add_fusion
  10.4 0.1 convert_reduce_fusion.1
  10.5 0.1 select_reduce_fusion.2.ends
  10.6 0.1 select_reduce_fusion.1
  10.7 0.2 convert_reduce_fusion
  11.0 0.2 select_reduce_fusion
  11.2 0.1 pad.1.clone
  11.3 1.3 %pad_maximum_fusion.local.amps = bf16[25,128,128]{2,1,0:T(8,128)(2,1)S(1)} fusion(bf16[8,128,128]{2,1,0:T(8,128)(2,1)} %param.6, bf16[16,128,128]{2,1,0:T(8,128)(2,1)} %param.5, bf16[25]{0:T(256)(128)(2,1)S(1)} %pad.1.clone), kind=kLoop, calls=%fused_computation | loop fusion | flops 819200 | bytes 1605682 | tf_op jit(solution)/shard_map/concatenate | solution.py:172
  12.5 0.1 convert_reduce_fusion.2.target
  12.6 2.7 %all-to-all-done.wanted = s32[16,4,16]{2,1,0:T(4,128)S(1)} async-done(((s32[16,4,16]{2,1,0:T(4,128)}), s32[16,4,16]{2,1,0:T(4,128)S(1)}, u32[]{:S(2)}, u32[]{:S(2)}) %all-to-all-start) | async-done | bytes 4128 | tf_op jit(solution)/shard_map/all_to_all | solution.py:168
  15.3 1.2 %select.31 = bf16[64,128,128]{2,1,0:T(8,128)(2,1)S(1)} custom-call(s32[1]{0:T(128)} %bitcast.3.me, s32[16,4,16]{2,1,0:T(4,128)S(1)} %all-to-all-done.wanted, bf16[25,128,128]{2,1,0:T(8,128)(2,1)S(1)} %pad_maximum_fusion.local.amps), custom_call_target="tpu_custom_call" | custom-call | bytes 2097152 | tf_op jit(solution)/shard_map/select/pallas_call | solution.py:32
  16.6 28.7 %all_to_all.15.fetched = bf16[64,128,128]{2,1,0:T(8,128)(2,1)S(1)} all-to-all(bf16[64,128,128]{2,1,0:T(8,128)(2,1)S(1)} %select.31), channel_id=1, replica_groups=mesh['group'=16,'zh'=8,'zl'=2,'core'=2] {'group'}, dimensions={0} | all-to-all | bytes 4194304 | tf_op jit(solution)/shard_map/all_to_all | solution.py:174
  45.3 1.3 %contract_0.1 = f32[16,128,128]{2,1,0:T(8,128)S(1)} custom-call(s32[512]{0:T(512)S(1)} %broadcast_add_fusion.table, s32[256]{0:T(256)S(1)} %convert_reduce_fusion.2.target, s32[32]{0:T(128)S(1)} %select_reduce_fusion.2.ends, bf16[25,128,128]{2,1,0:T(8,128)(2,1)S(1)} %pad_maximum_fusion.local.amps, bf16[64,128,128]{2,1,0:T(8,128)(2,1)S(1)} %all_to_all.15.fetched), custom_call_target="tpu_custom_call" | custom-call | flops 4294967296 | bytes 4194304 | tf_op jit(solution)/shard_map/contract_0/pallas_call | solution.py:93
  46.5 6.3 %collective-permute-start = (f32[16,128,128]{2,1,0:T(8,128)S(1)}, f32[16,128,128]{2,1,0:T(8,128)S(1)}, u32[]{:S(2)}, u32[]{:S(2)}) collective-permute-start(f32[16,128,128]{2,1,0:T(8,128)S(1)} %contract_0.1), channel_id=1, source_target_pairs={{0,1},{1,0},{2,3},{3,2},{4,5},{5,4},{6,7},{7,6},{8,9},{9,8},{10,11... | collective-permute-start | bytes 3145736 | tf_op jit(solution)/shard_map/ppermute | solution.py:180
  52.9 1.1 %contract_16.1.own = f32[8,128,128]{2,1,0:T(8,128)S(1)} custom-call(s32[512]{0:T(512)S(1)} %broadcast_add_fusion.table, s32[256]{0:T(256)S(1)} %convert_reduce_fusion.2.target, s32[32]{0:T(128)S(1)} %select_reduce_fusion.2.ends, bf16[25,128,128]{2,1,0:T(8,128)(2,1)S(1)} %pad_maximum_fusion.local.amps, bf16[64,128,128]{2,1,0:T(8,128)(2,1)S(1)} %all_to_all.15.fetched), custom_call_target="tpu_custom_call" | custom-call | flops 4294967296 | bytes 4194304 | tf_op jit(solution)/shard_map/contract_16/pallas_call | solution.py:93
  54.0 1.2 %collective-permute-done.other = f32[16,128,128]{2,1,0:T(8,128)S(1)} collective-permute-done((f32[16,128,128]{2,1,0:T(8,128)S(1)}, f32[16,128,128]{2,1,0:T(8,128)S(1)}, u32[]{:S(2)}, u32[]{:S(2)}) %collective-permute-start) | collective-permute-done | bytes 1048608 | tf_op jit(solution)/shard_map/ppermute | solution.py:180
  55.1 0.2 give.1
  55.4 12.4 %collective-permute-start.1 = (s16[8,136,128]{2,1,0:T(8,128)(2,1)S(1)}, s16[8,136,128]{2,1,0:T(8,128)(2,1)S(1)}, u32[]{:S(2)}, u32[]{:S(2)}) collective-permute-start(s16[8,136,128]{2,1,0:T(8,128)(2,1)S(1)} %give.1), channel_id=1, source_target_pairs={{0,2},{1,31},{2,0},{3,5},{4,6},{5,3},{6,4},{7,9},{8,10},{9,7},{10,... | collective-permute-start | bytes 835592 | tf_op jit(solution)/shard_map/ppermute | solution.py:184
  67.8 1.1 %contract_24.1.own = f32[8,128,128]{2,1,0:T(8,128)S(1)} custom-call(s32[512]{0:T(512)S(1)} %broadcast_add_fusion.table, s32[256]{0:T(256)S(1)} %convert_reduce_fusion.2.target, s32[32]{0:T(128)S(1)} %select_reduce_fusion.2.ends, bf16[25,128,128]{2,1,0:T(8,128)(2,1)S(1)} %pad_maximum_fusion.local.amps, bf16[64,128,128]{2,1,0:T(8,128)(2,1)S(1)} %all_to_all.15.fetched), custom_call_target="tpu_custom_call" | custom-call | flops 4294967296 | bytes 4194304 | tf_op jit(solution)/shard_map/contract_24/pallas_call | solution.py:93
  68.9 2.8 %collective-permute-done.1.arrived = s16[8,136,128]{2,1,0:T(8,128)(2,1)S(1)} collective-permute-done((s16[8,136,128]{2,1,0:T(8,128)(2,1)S(1)}, s16[8,136,128]{2,1,0:T(8,128)(2,1)S(1)}, u32[]{:S(2)}, u32[]{:S(2)}) %collective-permute-start.1) | collective-permute-done | bytes 278560 | tf_op jit(solution)/shard_map/ppermute | solution.py:184
  71.7 0.3 take.1
  72.0 27.5 %all_to_all.16.pieces = s16[8,136,128]{2,1,0:T(8,128)(2,1)S(1)} all-to-all(s16[8,136,128]{2,1,0:T(8,128)(2,1)S(1)} %take.1), channel_id=1, replica_groups=mesh['group'=16,'zh'=8,'zl'=2,'core'=2] {'zh'}, dimensions={0} | all-to-all | bytes 557056 | tf_op jit(solution)/shard_map/all_to_all | solution.py:187
  99.4 0.7 finish.1
  (6 shorter events, 0.1 us)
Async XLA Ops:
  1.3 14.0 %all-to-all-start = ((s32[16,4,16]{2,1,0:T(4,128)}), s32[16,4,16]{2,1,0:T(4,128)S(1)}, u32[]{:S(2)}, u32[]{:S(2)}) async-start(s32[16,4,16]{2,1,0:T(4,128)} %broadcast_in_dim.66), calls=%async_computation | async-start | bytes 65536 | tf_op jit(solution)/shard_map/all_to_all | solution.py:168
  46.5 8.6 %collective-permute-start = (f32[16,128,128]{2,1,0:T(8,128)S(1)}, f32[16,128,128]{2,1,0:T(8,128)S(1)}, u32[]{:S(2)}, u32[]{:S(2)}) collective-permute-start(f32[16,128,128]{2,1,0:T(8,128)S(1)} %contract_0.1), channel_id=1, source_target_pairs={{0,1},{1,0},{2,3},{3,2},{4,5},{5,4},{6,7},{7,6},{8,9},{9,8},{10,11... | collective-permute-start | bytes 3145736 | tf_op jit(solution)/shard_map/ppermute | solution.py:180
  55.4 16.3 %collective-permute-start.1 = (s16[8,136,128]{2,1,0:T(8,128)(2,1)S(1)}, s16[8,136,128]{2,1,0:T(8,128)(2,1)S(1)}, u32[]{:S(2)}, u32[]{:S(2)}) collective-permute-start(s16[8,136,128]{2,1,0:T(8,128)(2,1)S(1)} %give.1), channel_id=1, source_target_pairs={{0,2},{1,31},{2,0},{3,5},{4,6},{5,3},{6,4},{7,9},{8,10},{9,7},{10,... | collective-permute-start | bytes 835592 | tf_op jit(solution)/shard_map/ppermute | solution.py:184
